TPU v7x, 256 devices: a whole 4x4x8 slice. The times are simulated.
256 devices in a mesh: section: 4 (over x), dp: 16 (over y_hi, z), tensor: 4 (over y_lo, core).
Axes of the slice: x: 4, y: 4 (y_hi: 2, y_lo: 2; y = y_hi * 2 + y_lo), z: 8, core: 2. Of those that a mesh axis runs over, the one named last changes fastest.
Arguments:
- enc_input: bfloat16 [2, 16, 128, 4096], P(None, 'dp', None, 'tensor'), may hold values from -10.8 to 10.8
- dec_input: bfloat16 [2, 16, 128, 4096], P(None, 'dp', None, 'tensor'), may hold values from -6 to 6
- lengths: int32 [2, 2, 16], P(None, None, 'dp'), may hold values from 16 to 128, as said below
- offset_bucket: int32 [2, 255], replicated, may hold values from 0 to 31
- bias_tables: float32 [2, 32, 32], P(None, None, 'tensor'), may hold values from -4.5 to 303
- norm_gain: float32 [4, 4096], P('section'), may hold values from 0.5 to 1.5
- final_gain: float32 [4096], P('tensor'), may hold values from 0.5 to 1.5
- w_query: bfloat16 [4, 4096, 2048], P('section', 'dp', 'tensor'), may hold values from -0.0234375 to 0.0234375
- w_key: bfloat16 [4, 4096, 2048], P('section', 'dp', 'tensor'), may hold values from -0.09375 to 0.09375
- w_value: bfloat16 [4, 4096, 2048], P('section', 'dp', 'tensor'), may hold values from -0.09375 to 0.09375
- w_out: bfloat16 [4, 2048, 4096], P('section', 'tensor', 'dp'), may hold values from -0.125 to 0.125
Outputs:
- section_out: bfloat16 [4, 2, 16, 128, 4096], P('section', None, 'dp', None, 'tensor')
Inputs may be any that keep to these rules, and one draw needn't show every extreme that they name: In every micro-batch, sequence 0 has both lengths equal to 128.
All inputs are finite; a program needn't handle non-finite values.
Results may differ from a plain program's by a relative error of at most 0.02.
Values may be sent and summed in bfloat16 or wider, within the bound.
No kernel may reach another device: no remote copies, remote signals or barrier semaphores. Data moves between devices by JAX's collectives and lax.ppermute only.
A program may use at most 128 MiB of HBM per device.

v0:
```python
import functools

import jax
import jax.numpy as jnp
from jax import lax
from jax.experimental import pallas as pl
from jax.experimental.pallas import tpu as pltpu
from jax.sharding import Mesh
from jax.sharding import PartitionSpec as P

D = 4096
HEAD_DIM = 64
ROWS = 256
BLOCKS = 16
IN_COLS = 768
L = 128
BF = jnp.bfloat16
F32 = jnp.float32


def z_shift(value, steps, sections):
    pairs = [(s * 8 + i, s * 8 + (i + steps) % 8) for s in sections for i in range(8)]
    return lax.ppermute(value, ("section", "z"), pairs)


def y_swap(value, mask, sections):
    pairs = [(s * 4 + i, s * 4 + (i ^ mask)) for s in sections for i in range(4)]
    return lax.ppermute(value, ("section", "yhi", "ylo"), pairs)


def core_swap(value, sections):
    pairs = [(s * 2 + i, s * 2 + 1 - i) for s in sections for i in range(2)]
    return lax.ppermute(value, ("section", "core"), pairs)


def hop(value, source, target):
    return lax.ppermute(value, "section", [(source, target)])


def pick(pair, index):
    return jnp.where(index == 0, pair[0], pair[1])


def arrange(first, second, gain_ref, meta, out_ref, seqs, lead):
    step = 16
    for a in range(seqs):

        def some_rows(r, carry, a=a):
            start = pl.multiple_of(r * step, step)
            chunks = []
            for f in range(4):
                source = first if f % 2 == 0 else second
                index = (a * 2 + f // 2,) if lead is None else (f // 2, lead)
                chunks.append(source[index + (pl.ds(start, step),)].astype(F32))
            square = sum(jnp.sum(c * c, axis=-1, keepdims=True) for c in chunks)
            scale = lax.rsqrt(square * (1.0 / D) + 1e-06)
            for f in range(4):
                normed = (chunks[f] * scale * gain_ref[f : f + 1, :]).astype(BF)
                for i in range(4):
                    place = pl.multiple_of(meta[f * 4 + i] * ROWS, ROWS)
                    out_ref[pl.ds(a * L + start, step), pl.ds(place, ROWS)] = normed[
                        :, i * ROWS : (i + 1) * ROWS
                    ]
            return carry

        lax.fori_loop(0, L // step, some_rows, 0)


def block_kernel(seqs, halves, cross, causal, at, on, meta, *rest):
    @pl.when(meta[on] != 0)
    def _():
        block_work(seqs, halves, cross, causal, at, meta, *rest)


def block_work(
    seqs, halves, cross, causal, at, meta, gain_ref, memory_gain, table, first, second, *rest
):
    blocks = rest[: halves * BLOCKS]
    keep, send = rest[halves * BLOCKS : halves * BLOCKS + 2]
    weights, rows, memory_rows, total, mixed, context, sems = rest[halves * BLOCKS + 2 :]
    copies = []
    for h in range(halves):
        for j in range(BLOCKS):
            copy = pltpu.make_async_copy(
                blocks[h * BLOCKS + j], weights.at[h, pl.ds(j * ROWS, ROWS), :], sems.at[h, j]
            )
            copy.start()
            copies.append(copy)
    arrange(first, second, gain_ref, meta, rows, seqs, 0 if cross else None)
    if cross:
        arrange(first, second, memory_gain, meta, memory_rows, seqs, 1)
    width = IN_COLS // 3
    pairs = width // L
    query_pos = lax.broadcasted_iota(jnp.int32, (L, L), 0)
    key_pos = lax.broadcasted_iota(jnp.int32, (L, L), 1)
    low = key_pos < HEAD_DIM
    reach = query_pos
    if causal is None:
        reach = query_pos + jnp.where(meta[32] == 0, L, 0)
    depth = 512

    for h in range(halves):
        for copy in copies[h * BLOCKS : (h + 1) * BLOCKS]:
            copy.wait()
        total[...] = jnp.zeros_like(total)

        def add_rows(k, carry, h=h):
            span = pl.ds(pl.multiple_of(k * depth, depth), depth)
            if cross:
                total[:, :width] += jnp.dot(
                    rows[:, span], weights[h, span, :width], preferred_element_type=F32
                )
                total[:, width:] += jnp.dot(
                    memory_rows[:, span],
                    weights[h, span, width:IN_COLS],
                    preferred_element_type=F32,
                )
            else:
                total[...] += jnp.dot(
                    rows[:, span], weights[h, span, :IN_COLS], preferred_element_type=F32
                )
            return carry

        lax.fori_loop(0, D // depth, add_rows, 0)
        mixed[...] = total[...].astype(BF)

        def two_heads(step, carry, h=h):
            a = step // pairs
            pair = step % pairs
            tokens = pl.ds(pl.multiple_of(a * L, L), L)
            q, k, v = (
                mixed[tokens, pl.ds(pl.multiple_of(s * width + pair * L, L), L)] for s in range(3)
            )
            nothing = jnp.zeros_like(q)
            both = jnp.concatenate([jnp.where(low, q, nothing), jnp.where(low, nothing, q)], axis=0)
            scores = lax.dot_general(both, k, (((1,), (1,)), ((), ())), preferred_element_type=F32)
            mask = key_pos < meta[at + a]
            if causal is not False:
                mask = jnp.logical_and(mask, key_pos <= reach)
            probs = []
            for n in range(2):
                part = scores[n * L : (n + 1) * L]
                if not cross:
                    line = table[pl.ds(h * 2 * pairs + pair * 2 + n, 1), :]
                    grid = pltpu.roll(
                        jnp.broadcast_to(line, (L, 2 * L)), L + 1, 1, stride=1, stride_axis=0
                    )
                    part = part + grid[:, :L]
                part = jnp.where(mask, part, -1e30)
                power = jnp.exp(part - jnp.max(part, axis=-1, keepdims=True))
                probs.append((power / jnp.sum(power, axis=-1, keepdims=True)).astype(BF))
            out = jnp.dot(jnp.concatenate(probs, axis=0), v, preferred_element_type=F32)
            context[tokens, pl.ds(pl.multiple_of(h * width + pair * L, L), L)] = jnp.where(
                low, out[:L], out[L:]
            ).astype(BF)
            return carry

        lax.fori_loop(0, seqs * pairs, two_heads, 0)

    def out_block(j, carry):
        span = pl.ds(pl.multiple_of(j * ROWS, ROWS), ROWS)
        term = None
        for h in range(halves):
            one = jnp.dot(
                context[:, h * width : (h + 1) * width],
                weights[h, span, IN_COLS:],
                preferred_element_type=F32,
            )
            term = one if term is None else term + one
        term = term.astype(BF)
        slot = meta[16 + j]
        columns = pl.ds(pl.multiple_of((slot & 3) * ROWS, ROWS), ROWS)
        for side, out in ((0, keep), (1, send)):

            @pl.when(((slot >> 2) & 1) == side)
            def _():
                for a in range(seqs):
                    out[a * 2 + (slot >> 3), :, columns] = term[a * L : (a + 1) * L]

        return carry

    lax.fori_loop(0, BLOCKS, out_block, 0)


def run_block(meta, at, on, gain, memory_gain, table, first, second, blocks, seqs, cross, causal):
    halves = len(blocks) // BLOCKS
    tokens = seqs * L
    shape = jax.ShapeDtypeStruct((2 * seqs, L, D // 4), BF)
    in_vmem = pl.BlockSpec(memory_space=pltpu.VMEM)
    flops = 2 * tokens * D * 1024 * halves
    return pl.pallas_call(
        functools.partial(block_kernel, seqs, halves, cross, causal, at, on),
        out_shape=(shape, shape),
        in_specs=[pl.BlockSpec(memory_space=pltpu.SMEM)]
        + [in_vmem] * 5
        + [pl.BlockSpec(memory_space=pl.ANY)] * len(blocks),
        out_specs=(in_vmem, in_vmem),
        scratch_shapes=[
            pltpu.VMEM((halves, BLOCKS * ROWS, 1024), BF),
            pltpu.VMEM((tokens, D), BF),
            pltpu.VMEM((tokens, D) if cross else (16, 128), BF),
            pltpu.VMEM((tokens, IN_COLS), F32),
            pltpu.VMEM((tokens, IN_COLS), BF),
            pltpu.VMEM((tokens, halves * IN_COLS // 3), BF),
            pltpu.SemaphoreType.DMA((halves, BLOCKS)),
        ],
        compiler_params=pltpu.CompilerParams(vmem_limit_bytes=48 * 1024 * 1024),
        cost_estimate=pl.CostEstimate(
            flops=flops,
            bytes_accessed=len(blocks) * ROWS * 2048 + 8 * tokens * D,
            transcendentals=0,
        ),
    )(meta, gain, memory_gain, table, first, second, *blocks)


def ring(own, right, left, sections):
    ahead, behind = [own], []
    for k in range(max(right, left)):
        if k < right:
            ahead.append(z_shift(ahead[-1], 1, sections))
        if k < left:
            last = behind[-1] if behind else own
            behind.append(z_shift(last, -1, sections))
    return ahead + behind[::-1]


def body(
    enc_input,
    dec_input,
    lengths,
    offset_bucket,
    bias_tables,
    norm_gain,
    final_gain,
    w_query,
    w_key,
    w_value,
    w_out,
):
    section_id = lax.axis_index("section")
    yhi, z = lax.axis_index("yhi"), lax.axis_index("z")
    ylo, core = lax.axis_index("ylo"), lax.axis_index("core")
    micros, _, length, quarter = enc_input.shape
    hidden = w_query.shape[2] // 2
    everywhere = (0, 1, 2, 3)

    packs = [
        jnp.concatenate(
            [w[0, :, s : s + hidden] for w in (w_query, w_key, w_value)] + [w_out[0, s : s + hidden]],
            axis=1,
        )
        for s in (0, hidden)
    ]
    own = pick(packs, yhi)
    other = pick(packs, 1 - yhi)
    own, other = lax.optimization_barrier((own, other))
    crossed = y_swap(other, 2, everywhere)
    near_list = ring(own, 4, 3, everywhere)
    cross_list = ring(crossed, 3, 4, everywhere)
    half_one = near_list + cross_list
    far_own = ring(other, 4, 3, (2, 3))
    far_cross = ring(y_swap(own, 2, (2, 3)), 3, 4, (2, 3))
    half_two = far_own + far_cross

    slots = jnp.arange(BLOCKS, dtype=jnp.int32)
    flip = (slots >> 3) ^ ylo ^ yhi
    source = (((slots >> 2) & 1) ^ core) * 4 + (slots & 3)
    place = flip * 8 + ((z - source) & 7)
    flip_of = slots >> 3
    source_of = (z - (slots & 7)) & 7
    slot_of = (flip_of ^ yhi ^ ylo) * 8 + ((source_of >> 2) ^ core) * 4 + (source_of & 3)

    across_lengths = y_swap(lengths, 2, (0, 1))
    both_lengths = jnp.concatenate([lengths, across_lengths], axis=2)
    own_lengths = jnp.where(section_id == 0, both_lengths[:, 0], both_lengths[:, 1]).reshape(4)
    flag = (section_id != 0).astype(jnp.int32)[None]
    ticks = jnp.stack([section_id < 2, section_id == 2, section_id == 3]).astype(jnp.int32)
    meta = jnp.concatenate(
        [place, slot_of, flag, own_lengths, lengths[:, 0, 0], lengths[:, 1, 0], ticks]
    )

    bucket_row = jnp.where(section_id == 0, offset_bucket[0], offset_bucket[1])
    tables = jnp.where(section_id == 0, bias_tables[0], bias_tables[1])
    tables = pick((tables, jnp.roll(tables, 4, axis=1)), yhi)
    padded = jnp.concatenate([bucket_row, jnp.zeros((1,), jnp.int32)])
    table = jnp.zeros((tables.shape[1], 2 * length), F32)
    for bucket in range(tables.shape[0]):
        table = jnp.where(padded[None] == bucket, tables[bucket][:, None], table)

    gain = norm_gain[0].reshape(2, 2, quarter)
    gain = pick((gain, gain[::-1]), ylo)
    gain = pick((gain, gain[:, ::-1]), core).reshape(4, quarter)
    final_near = y_swap(final_gain, 1, (2,))
    final_two = jnp.stack([final_gain, final_near])
    final_whole = jnp.stack([final_two, core_swap(final_two, (2,))], axis=1).reshape(4, quarter)

    def summed(keep, got, index):
        return keep[index].astype(F32) + got[index].astype(F32)

    firsts, seconds, thirds = [], [], []
    secs = (0, 1)
    for micro in range(micros):
        piece = jnp.where(section_id == 0, enc_input[micro, 0], dec_input[micro, 0])
        stack = jnp.stack([piece] + [y_swap(piece, mask, secs) for mask in (1, 2, 3)])
        swapped = core_swap(stack, secs)
        keep, send = run_block(
            meta, 33 + 2 * micro, 41, gain, gain, table, stack, swapped, half_one, 2, False, None
        )
        got = core_swap(send, secs)
        attended = summed(keep, got, 0)
        for mask in (1, 2, 3):
            back = y_swap(summed(keep, got, mask).astype(BF), mask, secs)
            attended = attended + back.astype(F32)
        firsts.append((piece.astype(F32) + attended).astype(BF))

    def combine(piece, keep, send, secs):
        got = core_swap(send, secs)
        beside = y_swap(summed(keep, got, 1).astype(BF), 1, secs)
        return (piece.astype(F32) + summed(keep, got, 0) + beside.astype(F32)).astype(BF)

    for micro in range(micros):
        piece = hop(firsts[micro], 1, 2)
        both = jnp.stack([piece, hop(firsts[micro], 0, 2)])
        stack = jnp.stack([both, y_swap(both, 1, (2,))])
        swapped = core_swap(stack, (2,))
        blocks = half_one + half_two
        keep, send = run_block(
            meta, 37 + micro, 42, gain, final_whole, table, stack, swapped, blocks, 1, True, False
        )
        seconds.append(combine(piece, keep, send, (2,)))
    for micro in range(micros):
        piece = hop(seconds[micro], 2, 3)
        stack = jnp.stack([piece, y_swap(piece, 1, (3,))])
        swapped = core_swap(stack, (3,))
        blocks = half_one + half_two
        keep, send = run_block(
            meta, 39 + micro, 43, gain, gain, table, stack, swapped, blocks, 1, False, True
        )
        thirds.append(combine(piece, keep, send, (3,)))

    first = jnp.stack(firsts)
    wide = first.astype(F32)
    square = jnp.sum(wide * wide, axis=-1)
    square = square + core_swap(square, (0,))
    square = square + y_swap(square, 1, (0,))
    encoded = (wide * lax.rsqrt(square / D + 1e-06)[:, :, None] * final_gain).astype(BF)
    early = jnp.where(section_id == 0, encoded, first)
    result = jnp.stack(
        [
            jnp.where(
                section_id == 3, thirds[m], jnp.where(section_id == 2, seconds[m], early[m])
            )
            for m in range(micros)
        ]
    )
    return result[None, :, None]


def solution(mesh):
    sections, dp, tensor = (mesh.shape[name] for name in ("section", "dp", "tensor"))
    fine = Mesh(
        mesh.devices.reshape(sections, 2, dp // 2, tensor // 2, 2),
        ("section", "yhi", "z", "ylo", "core"),
    )
    dp, tensor = ("yhi", "z"), ("ylo", "core")
    in_specs = (
        P(None, dp, None, tensor),
        P(None, dp, None, tensor),
        P(None, None, dp),
        P(),
        P(None, None, tensor),
        P("section", None),
        P(tensor),
        P("section", dp, tensor),
        P("section", dp, tensor),
        P("section", dp, tensor),
        P("section", tensor, dp),
    )
    out_specs = P("section", None, dp, None, tensor)

    return jax.shard_map(body, mesh=fine, in_specs=in_specs, out_specs=out_specs, check_vma=False)
```

profile of v0, /device:TPU:6, one launch (start us, length us, event | category | flops | bytes accessed | tf_op | source)
XLA Modules:
  0.0 416.2 jit_solution(869601364694127985)
XLA Ops:
  16.8 5.9 %collective-permute-start.16 = (bf16[256,1024]{1,0:T(8,128)(2,1)S(1)}, bf16[256,1024]{1,0:T(8,128)(2,1)}, u32[]{:S(2)}, u32[]{:S(2)}) collective-permute-start(bf16[256,1024]{1,0:T(8,128)(2,1)S(1)} %collective-permute-done.12.rest_13_), channel_id=1, source_target_pairs={{0,28},{4,0},{8,4},{12,8},{16,12},{20,16},{24,20},{28,24},{64,92},... | collective-permute-start | bytes 1572872 | tf_op jit(solution)/shard_map/ppermute | solution.py:23
  31.5 3.5 collective-permute-done.16.rest_20_
  35.0 3.8 collective-permute-start.17
  39.7 6.5 %collective-permute-done.9.rest_12_ = bf16[256,1024]{1,0:T(8,128)(2,1)S(1)} collective-permute-done((bf16[256,1024]{1,0:T(8,128)(2,1)S(1)}, bf16[256,1024]{1,0:T(8,128)(2,1)S(1)}, u32[]{:S(2)}, u32[]{:S(2)}) %collective-permute-start.9) | collective-permute-done | bytes 524320 | tf_op jit(solution)/shard_map/ppermute | solution.py:23
  46.2 3.7 collective-permute-start.10
  51.3 6.3 %collective-permute-done.6.rest_7_ = bf16[256,1024]{1,0:T(8,128)(2,1)S(1)} collective-permute-done((bf16[256,1024]{1,0:T(8,128)(2,1)S(1)}, bf16[256,1024]{1,0:T(8,128)(2,1)S(1)}, u32[]{:S(2)}, u32[]{:S(2)}) %collective-permute-start.6) | collective-permute-done | bytes 524320 | tf_op jit(solution)/shard_map/ppermute | solution.py:23
  57.7 3.6 collective-permute-start.18
  64.9 3.8 collective-permute-done.10.rest_11_
  70.4 3.9 collective-permute-start.11
  74.3 6.0 %collective-permute-done.7.rest_8_ = bf16[256,1024]{1,0:T(8,128)(2,1)} collective-permute-done((bf16[256,1024]{1,0:T(8,128)(2,1)S(1)}, bf16[256,1024]{1,0:T(8,128)(2,1)}, u32[]{:S(2)}, u32[]{:S(2)}) %collective-permute-start.7) | collective-permute-done | bytes 524320 | tf_op jit(solution)/shard_map/ppermute | solution.py:23
  80.2 3.5 collective-permute-start.19
  87.3 4.0 collective-permute-done.11.rest_10_
  91.5 8.7 %collective-permute-done.8.rest_9_ = bf16[256,1024]{1,0:T(8,128)(2,1)} collective-permute-done((bf16[256,1024]{1,0:T(8,128)(2,1)}, bf16[256,1024]{1,0:T(8,128)(2,1)}, u32[]{:S(2)}, u32[]{:S(2)}) %collective-permute-start.8) | collective-permute-done | bytes 524320 | tf_op jit(solution)/shard_map/ppermute | solution.py:23
  108.4 5.6 %collective-permute-start.34 = (bf16[256,1024]{1,0:T(8,128)(2,1)S(1)}, bf16[256,1024]{1,0:T(8,128)(2,1)S(1)}, u32[]{:S(2)}, u32[]{:S(2)}) collective-permute-start(bf16[256,1024]{1,0:T(8,128)(2,1)S(1)} %copy-done.4), channel_id=1, source_target_pairs={{128,156},{132,128},{136,132},{140,136},{144,140},{148,144},{152,1... | collective-permute-start | bytes 1572872 | tf_op jit(solution)/shard_map/ppermute | solution.py:23
  117.1 5.1 %collective-permute-start.37 = (bf16[256,1024]{1,0:T(8,128)(2,1)S(1)}, bf16[256,1024]{1,0:T(8,128)(2,1)S(1)}, u32[]{:S(2)}, u32[]{:S(2)}) collective-permute-start(bf16[256,1024]{1,0:T(8,128)(2,1)S(1)} %get-tuple-element.19.rest_5_), channel_id=1, source_target_pairs={{128,160},{130,162},{160,128},{162,130},{192,224},{194,226},{224,1... | collective-permute-start | bytes 1572872 | tf_op jit(solution)/shard_map/ppermute | solution.py:28
  127.9 4.3 %collective-permute-done.37.rest_29_ = bf16[256,1024]{1,0:T(8,128)(2,1)S(1)} collective-permute-done((bf16[256,1024]{1,0:T(8,128)(2,1)S(1)}, bf16[256,1024]{1,0:T(8,128)(2,1)S(1)}, u32[]{:S(2)}, u32[]{:S(2)}) %collective-permute-start.37) | collective-permute-done | bytes 524320 | tf_op jit(solution)/shard_map/ppermute | solution.py:28
  145.0 3.6 collective-permute-start.38
  148.6 7.5 %collective-permute-done.41.rest_36_ = bf16[256,1024]{1,0:T(8,128)(2,1)S(1)} collective-permute-done((bf16[256,1024]{1,0:T(8,128)(2,1)S(1)}, bf16[256,1024]{1,0:T(8,128)(2,1)S(1)}, u32[]{:S(2)}, u32[]{:S(2)}) %collective-permute-start.41) | collective-permute-done | bytes 524320 | tf_op jit(solution)/shard_map/ppermute | solution.py:23
  156.1 3.7 collective-permute-start.42
  163.5 3.9 collective-permute-start.32
  172.8 4.9 %collective-permute-start.43 = (bf16[256,1024]{1,0:T(8,128)(2,1)S(1)}, bf16[256,1024]{1,0:T(8,128)(2,1)}, u32[]{:S(2)}, u32[]{:S(2)}) collective-permute-start(bf16[256,1024]{1,0:T(8,128)(2,1)S(1)} %collective-permute-done.42.rest_35_), channel_id=1, source_target_pairs={{128,156},{132,128},{136,132},{140,136},{144,140},{148,144},{152,1... | collective-permute-start | bytes 1572872 | tf_op jit(solution)/shard_map/ppermute | solution.py:23
  180.4 3.6 collective-permute-done.36.rest_26_
  187.6 5.2 %collective-permute-done.39.rest_31_ = bf16[256,1024]{1,0:T(8,128)(2,1)} collective-permute-done((bf16[256,1024]{1,0:T(8,128)(2,1)S(1)}, bf16[256,1024]{1,0:T(8,128)(2,1)}, u32[]{:S(2)}, u32[]{:S(2)}) %collective-permute-start.39) | collective-permute-done | bytes 524320 | tf_op jit(solution)/shard_map/ppermute | solution.py:23
  195.5 4.3 %collective-permute-start.44 = (bf16[256,1024]{1,0:T(8,128)(2,1)}, bf16[256,1024]{1,0:T(8,128)(2,1)}, u32[]{:S(2)}, u32[]{:S(2)}) collective-permute-start(bf16[256,1024]{1,0:T(8,128)(2,1)} %collective-permute-done.43.rest_34_), channel_id=1, source_target_pairs={{128,156},{132,128},{136,132},{140,136},{144,140},{148,144},{152,1... | collective-permute-start | bytes 1572872 | tf_op jit(solution)/shard_map/ppermute | solution.py:23
  199.9 4.1 collective-permute-done.33.rest_25_
  204.0 7.7 %collective-permute-done.40.rest_32_ = bf16[256,1024]{1,0:T(8,128)(2,1)} collective-permute-done((bf16[256,1024]{1,0:T(8,128)(2,1)}, bf16[256,1024]{1,0:T(8,128)(2,1)}, u32[]{:S(2)}, u32[]{:S(2)}) %collective-permute-start.40) | collective-permute-done | bytes 524320 | tf_op jit(solution)/shard_map/ppermute | solution.py:23
  221.9 126.9 %collective-permute-done.47 = bf16[128,1024]{1,0:T(8,128)(2,1)S(1)} collective-permute-done((bf16[128,1024]{1,0:T(8,128)(2,1)S(1)}, bf16[128,1024]{1,0:T(8,128)(2,1)S(1)}, u32[]{:S(2)}, u32[]{:S(2)}) %collective-permute-start.47) | collective-permute-done | bytes 262176 | tf_op jit(solution)/shard_map/ppermute | solution.py:37
  359.1 4.1 collective-permute-done.69
  365.1 13.6 %shard_map.111 = (bf16[2,128,1024]{2,1,0:T(8,128)(2,1)S(1)}, bf16[2,128,1024]{2,1,0:T(8,128)(2,1)S(1)}) custom-call(s32[44]{0:T(128)S(1)} %concatenate.150.meta, f32[4,1024]{1,0:T(4,128)S(1)} %reshape.595.rest_0_.rest_1_, f32[4,1024]{1,0:T(4,128)S(1)} %reshape.595.rest_0_.rest_1_, f32[8,256]{1,0:T(8,128)S(1)} %select_select_fusion.rest_2_, ...), custom_call_target="tpu_custom_call" | custom-call | flops 2147483648 | bytes 20971520 | tf_op jit(solution)/shard_map/pallas_call | solution.py:191
  381.3 13.6 %shard_map.114 = (bf16[2,128,1024]{2,1,0:T(8,128)(2,1)S(1)}, bf16[2,128,1024]{2,1,0:T(8,128)(2,1)S(1)}) custom-call(s32[44]{0:T(128)S(1)} %concatenate.150.meta, f32[4,1024]{1,0:T(4,128)S(1)} %reshape.595.rest_0_.rest_1_, f32[4,1024]{1,0:T(4,128)S(1)} %reshape.595.rest_0_.rest_1_, f32[8,256]{1,0:T(8,128)S(1)} %select_select_fusion.rest_2_, ...), custom_call_target="tpu_custom_call" | custom-call | flops 2147483648 | bytes 20971520 | tf_op jit(solution)/shard_map/pallas_call | solution.py:191
  404.8 4.9 %collective-permute-done.51 = bf16[128,1024]{1,0:T(8,128)(2,1)S(1)} collective-permute-done((bf16[128,1024]{1,0:T(8,128)(2,1)S(1)}, bf16[128,1024]{1,0:T(8,128)(2,1)S(1)}, u32[]{:S(2)}, u32[]{:S(2)}) %collective-permute-start.51) | collective-permute-done | bytes 262176 | tf_op jit(solution)/shard_map/ppermute | solution.py:28
  409.6 5.1 %collective-permute-done.72 = bf16[128,1024]{1,0:T(8,128)(2,1)S(1)} collective-permute-done((bf16[128,1024]{1,0:T(8,128)(2,1)S(1)}, bf16[128,1024]{1,0:T(8,128)(2,1)S(1)}, u32[]{:S(2)}, u32[]{:S(2)}) %collective-permute-start.72) | collective-permute-done | bytes 262176 | tf_op jit(solution)/shard_map/ppermute | solution.py:28
  (285 shorter events, 119.9 us)
Async XLA Ops:
  12.9 18.5 %collective-permute-start.5 = (bf16[256,1024]{1,0:T(8,128)(2,1)S(1)}, bf16[256,1024]{1,0:T(8,128)(2,1)S(1)}, u32[]{:S(2)}, u32[]{:S(2)}) collective-permute-start(bf16[256,1024]{1,0:T(8,128)(2,1)S(1)} %get-tuple-element.19.rest_5_), channel_id=1, source_target_pairs={{0,4},{4,8},{8,12},{12,16},{16,20},{20,24},{24,28},{28,0},{64,68},... | collective-permute-start | bytes 1572872 | tf_op jit(solution)/shard_map/ppermute | solution.py:23
  16.8 18.2 %collective-permute-start.16 = (bf16[256,1024]{1,0:T(8,128)(2,1)S(1)}, bf16[256,1024]{1,0:T(8,128)(2,1)}, u32[]{:S(2)}, u32[]{:S(2)}) collective-permute-start(bf16[256,1024]{1,0:T(8,128)(2,1)S(1)} %collective-permute-done.12.rest_13_), channel_id=1, source_target_pairs={{0,28},{4,0},{8,4},{12,8},{16,12},{20,16},{24,20},{28,24},{64,92},... | collective-permute-start | bytes 1572872 | tf_op jit(solution)/shard_map/ppermute | solution.py:23
  25.4 20.8 %collective-permute-start.9 = (bf16[256,1024]{1,0:T(8,128)(2,1)S(1)}, bf16[256,1024]{1,0:T(8,128)(2,1)S(1)}, u32[]{:S(2)}, u32[]{:S(2)}) collective-permute-start(bf16[256,1024]{1,0:T(8,128)(2,1)S(1)} %get-tuple-element.19.rest_5_), channel_id=1, source_target_pairs={{0,28},{4,0},{8,4},{12,8},{16,12},{20,16},{24,20},{28,24},{64,92},... | collective-permute-start | bytes 1572872 | tf_op jit(solution)/shard_map/ppermute | solution.py:23
  28.8 41.6 %collective-permute-start.4 = (bf16[4,128,1024]{2,1,0:T(8,128)(2,1)}, bf16[4,128,1024]{2,1,0:T(8,128)(2,1)}, u32[]{:S(2)}, u32[]{:S(2)}) collective-permute-start(bf16[4,128,1024]{2,1,0:T(8,128)(2,1)} %pad_maximum_fusion.rest_3_), channel_id=1, source_target_pairs={{0,1},{1,0},{64,65},{65,64},{2,3},{3,2},{66,67},{67,66},{4,5},{5,4... | collective-permute-start | bytes 3145736 | tf_op jit(solution)/shard_map/ppermute | solution.py:33
  30.4 20.9 %collective-permute-start.13 = (bf16[256,1024]{1,0:T(8,128)(2,1)S(1)}, bf16[256,1024]{1,0:T(8,128)(2,1)S(1)}, u32[]{:S(2)}, u32[]{:S(2)}) collective-permute-start(bf16[256,1024]{1,0:T(8,128)(2,1)S(1)} %collective-permute-done.12.rest_13_), channel_id=1, source_target_pairs={{0,4},{4,8},{8,12},{12,16},{16,20},{20,24},{24,28},{28,0},{64,68},... | collective-permute-start | bytes 1572872 | tf_op jit(solution)/shard_map/ppermute | solution.py:23
  31.4 26.2 %collective-permute-start.6 = (bf16[256,1024]{1,0:T(8,128)(2,1)S(1)}, bf16[256,1024]{1,0:T(8,128)(2,1)S(1)}, u32[]{:S(2)}, u32[]{:S(2)}) collective-permute-start(bf16[256,1024]{1,0:T(8,128)(2,1)S(1)} %collective-permute-done.5.rest_6_), channel_id=1, source_target_pairs={{0,4},{4,8},{8,12},{12,16},{16,20},{20,24},{24,28},{28,0},{64,68},... | collective-permute-start | bytes 1572872 | tf_op jit(solution)/shard_map/ppermute | solution.py:23
  35.0 22.6 %collective-permute-start.17 = (bf16[256,1024]{1,0:T(8,128)(2,1)}, bf16[256,1024]{1,0:T(8,128)(2,1)}, u32[]{:S(2)}, u32[]{:S(2)}) collective-permute-start(bf16[256,1024]{1,0:T(8,128)(2,1)} %collective-permute-done.16.rest_20_), channel_id=1, source_target_pairs={{0,28},{4,0},{8,4},{12,8},{16,12},{20,16},{24,20},{28,24},{64,92},... | collective-permute-start | bytes 1572872 | tf_op jit(solution)/shard_map/ppermute | solution.py:23
  46.2 22.5 %collective-permute-start.10 = (bf16[256,1024]{1,0:T(8,128)(2,1)S(1)}, bf16[256,1024]{1,0:T(8,128)(2,1)}, u32[]{:S(2)}, u32[]{:S(2)}) collective-permute-start(bf16[256,1024]{1,0:T(8,128)(2,1)S(1)} %collective-permute-done.9.rest_12_), channel_id=1, source_target_pairs={{0,28},{4,0},{8,4},{12,8},{16,12},{20,16},{24,20},{28,24},{64,92},... | collective-permute-start | bytes 1572872 | tf_op jit(solution)/shard_map/ppermute | solution.py:23
  51.3 23.0 %collective-permute-start.14 = (bf16[256,1024]{1,0:T(8,128)(2,1)S(1)}, bf16[256,1024]{1,0:T(8,128)(2,1)}, u32[]{:S(2)}, u32[]{:S(2)}) collective-permute-start(bf16[256,1024]{1,0:T(8,128)(2,1)S(1)} %collective-permute-done.13.rest_14_), channel_id=1, source_target_pairs={{0,4},{4,8},{8,12},{12,16},{16,20},{20,24},{24,28},{28,0},{64,68},... | collective-permute-start | bytes 1572872 | tf_op jit(solution)/shard_map/ppermute | solution.py:23
  57.6 22.6 %collective-permute-start.7 = (bf16[256,1024]{1,0:T(8,128)(2,1)S(1)}, bf16[256,1024]{1,0:T(8,128)(2,1)}, u32[]{:S(2)}, u32[]{:S(2)}) collective-permute-start(bf16[256,1024]{1,0:T(8,128)(2,1)S(1)} %collective-permute-done.6.rest_7_), channel_id=1, source_target_pairs={{0,4},{4,8},{8,12},{12,16},{16,20},{20,24},{24,28},{28,0},{64,68},... | collective-permute-start | bytes 1572872 | tf_op jit(solution)/shard_map/ppermute | solution.py:23
  57.7 22.6 %collective-permute-start.18 = (bf16[256,1024]{1,0:T(8,128)(2,1)}, bf16[256,1024]{1,0:T(8,128)(2,1)}, u32[]{:S(2)}, u32[]{:S(2)}) collective-permute-start(bf16[256,1024]{1,0:T(8,128)(2,1)} %collective-permute-done.17.rest_19_), channel_id=1, source_target_pairs={{0,28},{4,0},{8,4},{12,8},{16,12},{20,16},{24,20},{28,24},{64,92},... | collective-permute-start | bytes 1572872 | tf_op jit(solution)/shard_map/ppermute | solution.py:23
  68.7 35.8 %collective-permute-start.55 = (bf16[4,128,1024]{2,1,0:T(8,128)(2,1)}, bf16[4,128,1024]{2,1,0:T(8,128)(2,1)}, u32[]{:S(2)}, u32[]{:S(2)}) collective-permute-start(bf16[4,128,1024]{2,1,0:T(8,128)(2,1)} %pad_maximum_fusion.2.rest_3_), channel_id=1, source_target_pairs={{0,1},{1,0},{64,65},{65,64},{2,3},{3,2},{66,67},{67,66},{4,5},{5,4... | collective-permute-start | bytes 3145736 | tf_op jit(solution)/shard_map/ppermute | solution.py:33
  70.4 20.9 %collective-permute-start.11 = (bf16[256,1024]{1,0:T(8,128)(2,1)}, bf16[256,1024]{1,0:T(8,128)(2,1)}, u32[]{:S(2)}, u32[]{:S(2)}) collective-permute-start(bf16[256,1024]{1,0:T(8,128)(2,1)} %collective-permute-done.10.rest_11_), channel_id=1, source_target_pairs={{0,28},{4,0},{8,4},{12,8},{16,12},{20,16},{24,20},{28,24},{64,92},... | collective-permute-start | bytes 1572872 | tf_op jit(solution)/shard_map/ppermute | solution.py:23
  80.2 19.9 %collective-permute-start.8 = (bf16[256,1024]{1,0:T(8,128)(2,1)}, bf16[256,1024]{1,0:T(8,128)(2,1)}, u32[]{:S(2)}, u32[]{:S(2)}) collective-permute-start(bf16[256,1024]{1,0:T(8,128)(2,1)} %collective-permute-done.7.rest_8_), channel_id=1, source_target_pairs={{0,4},{4,8},{8,12},{12,16},{16,20},{20,24},{24,28},{28,0},{64,68},... | collective-permute-start | bytes 1572872 | tf_op jit(solution)/shard_map/ppermute | solution.py:23
  80.2 20.3 %collective-permute-start.19 = (bf16[256,1024]{1,0:T(8,128)(2,1)}, bf16[256,1024]{1,0:T(8,128)(2,1)}, u32[]{:S(2)}, u32[]{:S(2)}) collective-permute-start(bf16[256,1024]{1,0:T(8,128)(2,1)} %collective-permute-done.18.rest_18_), channel_id=1, source_target_pairs={{0,28},{4,0},{8,4},{12,8},{16,12},{20,16},{24,20},{28,24},{64,92},... | collective-permute-start | bytes 1572872 | tf_op jit(solution)/shard_map/ppermute | solution.py:23
  132.2 27.6 %collective-permute-start.35 = (bf16[256,1024]{1,0:T(8,128)(2,1)S(1)}, bf16[256,1024]{1,0:T(8,128)(2,1)S(1)}, u32[]{:S(2)}, u32[]{:S(2)}) collective-permute-start(bf16[256,1024]{1,0:T(8,128)(2,1)S(1)} %collective-permute-done.34.rest_28_), channel_id=1, source_target_pairs={{128,156},{132,128},{136,132},{140,136},{144,140},{148,144},{152,1... | collective-permute-start | bytes 1572872 | tf_op jit(solution)/shard_map/ppermute | solution.py:23
  134.4 21.7 %collective-permute-start.41 = (bf16[256,1024]{1,0:T(8,128)(2,1)S(1)}, bf16[256,1024]{1,0:T(8,128)(2,1)S(1)}, u32[]{:S(2)}, u32[]{:S(2)}) collective-permute-start(bf16[256,1024]{1,0:T(8,128)(2,1)S(1)} %collective-permute-done.37.rest_29_), channel_id=1, source_target_pairs={{128,156},{132,128},{136,132},{140,136},{144,140},{148,144},{152,1... | collective-permute-start | bytes 1572872 | tf_op jit(solution)/shard_map/ppermute | solution.py:23
  140.6 19.9 %collective-permute-start.28 = (bf16[2,128,1024]{2,1,0:T(8,128)(2,1)S(1)}, bf16[2,128,1024]{2,1,0:T(8,128)(2,1)S(1)}, u32[]{:S(2)}, u32[]{:S(2)}) collective-permute-start(bf16[2,128,1024]{2,1,0:T(8,128)(2,1)S(1)} %get-tuple-element.82), channel_id=1, source_target_pairs={{128,130},{130,128},{160,162},{162,160},{129,131},{131,129},{161,1... | collective-permute-start | bytes 1572872 | tf_op jit(solution)/shard_map/ppermute | solution.py:28
  142.1 21.5 %collective-permute-start.31 = (bf16[256,1024]{1,0:T(8,128)(2,1)S(1)}, bf16[256,1024]{1,0:T(8,128)(2,1)S(1)}, u32[]{:S(2)}, u32[]{:S(2)}) collective-permute-start(bf16[256,1024]{1,0:T(8,128)(2,1)S(1)} %collective-permute-done.30.rest_22_), channel_id=1, source_target_pairs={{128,132},{132,136},{136,140},{140,144},{144,148},{148,152},{152,1... | collective-permute-start | bytes 1572872 | tf_op jit(solution)/shard_map/ppermute | solution.py:23
  145.0 23.0 %collective-permute-start.38 = (bf16[256,1024]{1,0:T(8,128)(2,1)S(1)}, bf16[256,1024]{1,0:T(8,128)(2,1)S(1)}, u32[]{:S(2)}, u32[]{:S(2)}) collective-permute-start(bf16[256,1024]{1,0:T(8,128)(2,1)S(1)} %collective-permute-done.37.rest_29_), channel_id=1, source_target_pairs={{128,132},{132,136},{136,140},{140,144},{144,148},{148,152},{152,1... | collective-permute-start | bytes 1572872 | tf_op jit(solution)/shard_map/ppermute | solution.py:23
  160.5 23.5 %collective-permute-start.36 = (bf16[256,1024]{1,0:T(8,128)(2,1)S(1)}, bf16[256,1024]{1,0:T(8,128)(2,1)S(1)}, u32[]{:S(2)}, u32[]{:S(2)}) collective-permute-start(bf16[256,1024]{1,0:T(8,128)(2,1)S(1)} %collective-permute-done.35.rest_27_), channel_id=1, source_target_pairs={{128,156},{132,128},{136,132},{140,136},{144,140},{148,144},{152,1... | collective-permute-start | bytes 1572872 | tf_op jit(solution)/shard_map/ppermute | solution.py:23
  163.5 22.1 %collective-permute-start.32 = (bf16[256,1024]{1,0:T(8,128)(2,1)S(1)}, bf16[256,1024]{1,0:T(8,128)(2,1)}, u32[]{:S(2)}, u32[]{:S(2)}) collective-permute-start(bf16[256,1024]{1,0:T(8,128)(2,1)S(1)} %collective-permute-done.31.rest_23_), channel_id=1, source_target_pairs={{128,132},{132,136},{136,140},{140,144},{144,148},{148,152},{152,1... | collective-permute-start | bytes 1572872 | tf_op jit(solution)/shard_map/ppermute | solution.py:23
  167.9 24.8 %collective-permute-start.39 = (bf16[256,1024]{1,0:T(8,128)(2,1)S(1)}, bf16[256,1024]{1,0:T(8,128)(2,1)}, u32[]{:S(2)}, u32[]{:S(2)}) collective-permute-start(bf16[256,1024]{1,0:T(8,128)(2,1)S(1)} %collective-permute-done.38.rest_30_), channel_id=1, source_target_pairs={{128,132},{132,136},{136,140},{140,144},{144,148},{148,152},{152,1... | collective-permute-start | bytes 1572872 | tf_op jit(solution)/shard_map/ppermute | solution.py:23
  172.8 22.7 %collective-permute-start.43 = (bf16[256,1024]{1,0:T(8,128)(2,1)S(1)}, bf16[256,1024]{1,0:T(8,128)(2,1)}, u32[]{:S(2)}, u32[]{:S(2)}) collective-permute-start(bf16[256,1024]{1,0:T(8,128)(2,1)S(1)} %collective-permute-done.42.rest_35_), channel_id=1, source_target_pairs={{128,156},{132,128},{136,132},{140,136},{144,140},{148,144},{152,1... | collective-permute-start | bytes 1572872 | tf_op jit(solution)/shard_map/ppermute | solution.py:23
  177.7 34.0 %collective-permute-start.29 = (bf16[2,2,128,1024]{3,2,1,0:T(8,128)(2,1)}, bf16[2,2,128,1024]{3,2,1,0:T(8,128)(2,1)}, u32[]{:S(2)}, u32[]{:S(2)}) collective-permute-start(bf16[2,2,128,1024]{3,2,1,0:T(8,128)(2,1)} %pad_maximum_fusion.1.rest_3_), channel_id=1, source_target_pairs={{128,129},{129,128},{130,131},{131,130},{132,133},{133,132},{134,1... | collective-permute-start | bytes 3145736 | tf_op jit(solution)/shard_map/ppermute | solution.py:33
  184.0 30.3 %collective-permute-start.65 = (bf16[2,2,128,1024]{3,2,1,0:T(8,128)(2,1)}, bf16[2,2,128,1024]{3,2,1,0:T(8,128)(2,1)}, u32[]{:S(2)}, u32[]{:S(2)}) collective-permute-start(bf16[2,2,128,1024]{3,2,1,0:T(8,128)(2,1)} %pad_maximum_fusion.3.rest_3_), channel_id=1, source_target_pairs={{128,129},{129,128},{130,131},{131,130},{132,133},{133,132},{134,1... | collective-permute-start | bytes 3145736 | tf_op jit(solution)/shard_map/ppermute | solution.py:33
  185.7 18.3 %collective-permute-start.33 = (bf16[256,1024]{1,0:T(8,128)(2,1)}, bf16[256,1024]{1,0:T(8,128)(2,1)}, u32[]{:S(2)}, u32[]{:S(2)}) collective-permute-start(bf16[256,1024]{1,0:T(8,128)(2,1)} %collective-permute-done.32.rest_24_), channel_id=1, source_target_pairs={{128,132},{132,136},{136,140},{140,144},{144,148},{148,152},{152,1... | collective-permute-start | bytes 1572872 | tf_op jit(solution)/shard_map/ppermute | solution.py:23
  192.8 18.9 %collective-permute-start.40 = (bf16[256,1024]{1,0:T(8,128)(2,1)}, bf16[256,1024]{1,0:T(8,128)(2,1)}, u32[]{:S(2)}, u32[]{:S(2)}) collective-permute-start(bf16[256,1024]{1,0:T(8,128)(2,1)} %collective-permute-done.39.rest_31_), channel_id=1, source_target_pairs={{128,132},{132,136},{136,140},{140,144},{144,148},{148,152},{152,1... | collective-permute-start | bytes 1572872 | tf_op jit(solution)/shard_map/ppermute | solution.py:23
  219.1 129.7 %collective-permute-start.47 = (bf16[128,1024]{1,0:T(8,128)(2,1)S(1)}, bf16[128,1024]{1,0:T(8,128)(2,1)S(1)}, u32[]{:S(2)}, u32[]{:S(2)}) collective-permute-start(bf16[128,1024]{1,0:T(8,128)(2,1)S(1)} %fusion.15), channel_id=1, source_target_pairs={{128,192},{129,193},{130,194},{131,195},{132,196},{133,197},{134,1... | collective-permute-start | bytes 786440 | tf_op jit(solution)/shard_map/ppermute | solution.py:37
  220.6 133.8 %collective-permute-start.68 = (bf16[128,1024]{1,0:T(8,128)(2,1)S(1)}, bf16[128,1024]{1,0:T(8,128)(2,1)S(1)}, u32[]{:S(2)}, u32[]{:S(2)}) collective-permute-start(bf16[128,1024]{1,0:T(8,128)(2,1)S(1)} %fusion.7), channel_id=1, source_target_pairs={{128,192},{129,193},{130,194},{131,195},{132,196},{133,197},{134,1... | collective-permute-start | bytes 786440 | tf_op jit(solution)/shard_map/ppermute | solution.py:37
  363.2 18.1 %collective-permute-start.70 = (bf16[2,128,1024]{2,1,0:T(8,128)(2,1)S(1)}, bf16[2,128,1024]{2,1,0:T(8,128)(2,1)S(1)}, u32[]{:S(2)}, u32[]{:S(2)}) collective-permute-start(bf16[2,128,1024]{2,1,0:T(8,128)(2,1)S(1)} %pad_maximum_fusion.10.rest_3_), channel_id=1, source_target_pairs={{192,193},{193,192},{194,195},{195,194},{196,197},{197,196},{198,1... | collective-permute-start | bytes 1572872 | tf_op jit(solution)/shard_map/ppermute | solution.py:33
  378.8 19.7 %collective-permute-start.50 = (bf16[2,128,1024]{2,1,0:T(8,128)(2,1)S(1)}, bf16[2,128,1024]{2,1,0:T(8,128)(2,1)S(1)}, u32[]{:S(2)}, u32[]{:S(2)}) collective-permute-start(bf16[2,128,1024]{2,1,0:T(8,128)(2,1)S(1)} %get-tuple-element.26), channel_id=1, source_target_pairs={{192,193},{193,192},{194,195},{195,194},{196,197},{197,196},{198,1... | collective-permute-start | bytes 1572872 | tf_op jit(solution)/shard_map/ppermute | solution.py:33
  (95 other events, 1080.7 us)
where the time goes:
time: 418 us; the launch traced here: 416 us
  waiting for transfers between devices  222 us (53%)
  starting transfers between devices  133 us (32%)
  Pallas kernels  37.2 us (9%)
  other arithmetic  15.6 us (4%)
  local copies, waits for them, and re-layouts  6.74 us (2%)
    ppermute x6, waiting for transfers between devices, hop(): return lax.ppermute(value, 'section', [(source, target)])  130 us
    ppermute x28, starting transfers between devices, z_shift(): return lax.ppermute(value, ('section', 'z'), pairs)  73.1 us
    ppermute x28, waiting for transfers between devices, z_shift(): return lax.ppermute(value, ('section', 'z'), pairs)  71.7 us
    pallas_call x6, Pallas kernels, run_block(): pl.pallas_call(functools.partial(block_kernel, seqs, halves, cross, causa...  37.2 us
    ppermute x25, starting transfers between devices, y_swap(): return lax.ppermute(value, ('section', 'yhi', 'ylo'), pairs)  35.1 us
    ppermute x25, waiting for transfers between devices, y_swap(): return lax.ppermute(value, ('section', 'yhi', 'ylo'), pairs)  20.5 us
    ppermute x14, starting transfers between devices, core_swap(): return lax.ppermute(value, ('section', 'core'), pairs)  19.4 us
  transfers between devices with their start and end apart: 73, of which 25 were waited for; matrix products, arithmetic and copies ran while one was open for 4% of the time, Pallas kernels for 9%

commit v1 on v0

--- a/solution.py
+++ b/solution.py
@@ -66,27 +66,60 @@
         lax.fori_loop(0, L // step, some_rows, 0)
 
 
-def block_kernel(seqs, halves, cross, causal, at, on, meta, *rest):
+def prepare_kernel(seqs, meta, gain_ref, first, second, rows):
+    @pl.when(meta[41] != 0)
+    def _():
+        arrange(first, second, gain_ref, meta, rows, seqs, None)
+
+
+def prepare(meta, gain, first, second, seqs):
+    in_vmem = pl.BlockSpec(memory_space=pltpu.VMEM)
+    return pl.pallas_call(
+        functools.partial(prepare_kernel, seqs),
+        out_shape=jax.ShapeDtypeStruct((seqs * L, D), BF),
+        in_specs=[pl.BlockSpec(memory_space=pltpu.SMEM)] + [in_vmem] * 3,
+        out_specs=in_vmem,
+        compiler_params=pltpu.CompilerParams(vmem_limit_bytes=16 * 1024 * 1024),
+        cost_estimate=pl.CostEstimate(
+            flops=8 * seqs * L * D, bytes_accessed=4 * seqs * L * D, transcendentals=0
+        ),
+    )(meta, gain, first, second)
+
+
+def block_kernel(seqs, halves, cross, causal, ready, at, on, meta, *rest):
     @pl.when(meta[on] != 0)
     def _():
-        block_work(seqs, halves, cross, causal, at, meta, *rest)
+        block_work(seqs, halves, cross, causal, ready, at, meta, *rest)
 
 
 def block_work(
-    seqs, halves, cross, causal, at, meta, gain_ref, memory_gain, table, first, second, *rest
+    seqs, halves, cross, causal, ready, at, meta, gain_ref, memory_gain, table, first, second, *rest
 ):
     blocks = rest[: halves * BLOCKS]
     keep, send = rest[halves * BLOCKS : halves * BLOCKS + 2]
-    weights, rows, memory_rows, total, mixed, context, sems = rest[halves * BLOCKS + 2 :]
-    copies = []
+    weights, rows, memory_rows, total, mixed, context, here, partial = rest[
+        halves * BLOCKS + 2 : halves * BLOCKS + 10
+    ]
+    sems, here_sems, exit_sems = rest[halves * BLOCKS + 10 :]
+    if ready:
+        entries = [pltpu.make_async_copy(first, rows, here_sems.at[0])]
+    else:
+        entries = [
+            pltpu.make_async_copy(source, here.at[n], here_sems.at[n])
+            for n, source in enumerate((first, second))
+        ]
+    for entry in entries:
+        entry.start()
     for h in range(halves):
         for j in range(BLOCKS):
-            copy = pltpu.make_async_copy(
+            pltpu.make_async_copy(
                 blocks[h * BLOCKS + j], weights.at[h, pl.ds(j * ROWS, ROWS), :], sems.at[h, j]
-            )
-            copy.start()
-            copies.append(copy)
-    arrange(first, second, gain_ref, meta, rows, seqs, 0 if cross else None)
+            ).start()
+    for entry in entries:
+        entry.wait()
+    first, second = here.at[0], here.at[1]
+    if not ready:
+        arrange(first, second, gain_ref, meta, rows, seqs, 0 if cross else None)
     if cross:
         arrange(first, second, memory_gain, meta, memory_rows, seqs, 1)
     width = IN_COLS // 3
@@ -97,15 +130,17 @@
     reach = query_pos
     if causal is None:
         reach = query_pos + jnp.where(meta[32] == 0, L, 0)
-    depth = 512
+    depth = 1024
 
     for h in range(halves):
-        for copy in copies[h * BLOCKS : (h + 1) * BLOCKS]:
-            copy.wait()
         total[...] = jnp.zeros_like(total)
 
         def add_rows(k, carry, h=h):
             span = pl.ds(pl.multiple_of(k * depth, depth), depth)
+            for b in range(depth // ROWS):
+                j = k * (depth // ROWS) + b
+                landed = weights.at[h, pl.ds(pl.multiple_of(j * ROWS, ROWS), ROWS), :]
+                pltpu.make_async_copy(landed, landed, sems.at[h, j]).wait()
             if cross:
                 total[:, :width] += jnp.dot(
                     rows[:, span], weights[h, span, :width], preferred_element_type=F32
@@ -155,7 +190,7 @@
             ).astype(BF)
             return carry
 
-        lax.fori_loop(0, seqs * pairs, two_heads, 0)
+        lax.fori_loop(0, seqs * pairs, two_heads, 0, unroll=2)
 
     def out_block(j, carry):
         span = pl.ds(pl.multiple_of(j * ROWS, ROWS), ROWS)
@@ -170,31 +205,35 @@
         term = term.astype(BF)
         slot = meta[16 + j]
         columns = pl.ds(pl.multiple_of((slot & 3) * ROWS, ROWS), ROWS)
-        for side, out in ((0, keep), (1, send)):
-
-            @pl.when(((slot >> 2) & 1) == side)
-            def _():
-                for a in range(seqs):
-                    out[a * 2 + (slot >> 3), :, columns] = term[a * L : (a + 1) * L]
-
+        for a in range(seqs):
+            partial[(slot >> 2) & 1, a * 2 + (slot >> 3), :, columns] = term[a * L : (a + 1) * L]
         return carry
 
-    lax.fori_loop(0, BLOCKS, out_block, 0)
+    lax.fori_loop(0, BLOCKS, out_block, 0, unroll=4)
+    exits = [
+        pltpu.make_async_copy(partial.at[side], target, exit_sems.at[side])
+        for side, target in ((1, send), (0, keep))
+    ]
+    for leave in exits:
+        leave.start()
+    for leave in exits:
+        leave.wait()
 
 
 def run_block(meta, at, on, gain, memory_gain, table, first, second, blocks, seqs, cross, causal):
     halves = len(blocks) // BLOCKS
     tokens = seqs * L
+    ready = first.ndim == 2
     shape = jax.ShapeDtypeStruct((2 * seqs, L, D // 4), BF)
     in_vmem = pl.BlockSpec(memory_space=pltpu.VMEM)
     flops = 2 * tokens * D * 1024 * halves
     return pl.pallas_call(
-        functools.partial(block_kernel, seqs, halves, cross, causal, at, on),
+        functools.partial(block_kernel, seqs, halves, cross, causal, ready, at, on),
         out_shape=(shape, shape),
         in_specs=[pl.BlockSpec(memory_space=pltpu.SMEM)]
-        + [in_vmem] * 5
-        + [pl.BlockSpec(memory_space=pl.ANY)] * len(blocks),
-        out_specs=(in_vmem, in_vmem),
+        + [in_vmem] * 3
+        + [pl.BlockSpec(memory_space=pl.ANY)] * (2 + len(blocks)),
+        out_specs=(pl.BlockSpec(memory_space=pl.ANY),) * 2,
         scratch_shapes=[
             pltpu.VMEM((halves, BLOCKS * ROWS, 1024), BF),
             pltpu.VMEM((tokens, D), BF),
@@ -202,7 +241,11 @@
             pltpu.VMEM((tokens, IN_COLS), F32),
             pltpu.VMEM((tokens, IN_COLS), BF),
             pltpu.VMEM((tokens, halves * IN_COLS // 3), BF),
+            pltpu.VMEM((2, 16, 128) if ready else (2,) + first.shape, BF),
+            pltpu.VMEM((2, 2 * seqs, L, D // 4), BF),
             pltpu.SemaphoreType.DMA((halves, BLOCKS)),
+            pltpu.SemaphoreType.DMA((2,)),
+            pltpu.SemaphoreType.DMA((2,)),
         ],
         compiler_params=pltpu.CompilerParams(vmem_limit_bytes=48 * 1024 * 1024),
         cost_estimate=pl.CostEstimate(
@@ -303,8 +346,9 @@
         piece = jnp.where(section_id == 0, enc_input[micro, 0], dec_input[micro, 0])
         stack = jnp.stack([piece] + [y_swap(piece, mask, secs) for mask in (1, 2, 3)])
         swapped = core_swap(stack, secs)
+        rows = prepare(meta, gain, stack, swapped, 2)
         keep, send = run_block(
-            meta, 33 + 2 * micro, 41, gain, gain, table, stack, swapped, half_one, 2, False, None
+            meta, 33 + 2 * micro, 41, gain, gain, table, rows, rows, half_one, 2, False, None
         )
         got = core_swap(send, secs)
         attended = summed(keep, got, 0)

time: 418 us -> 398 us (0.952)
  Pallas kernels: 37.2 us -> 24.7 us
  waiting for transfers between devices: 222 us -> 213 us
    pallas_call x6, Pallas kernels: 37.2 us -> 21.6 us  [run_block(): pl.pallas_call(functools.partial(block_kernel, seqs, halves, cross, causa...]
    ppermute x6, waiting for transfers between devices: 130 us -> 122 us  [hop(): return lax.ppermute(value, 'section', [(source, target)])]
  transfers between devices with their start and end apart: 73 -> 73, of which waited for: 25 -> 26; matrix products, arithmetic and copies ran while one was open for 4% -> 5% of each run, Pallas kernels for 9% -> 6%
where the time goes in v1:
time: 398 us; the launch traced here: 396 us
  waiting for transfers between devices  213 us (54%)
  starting transfers between devices  132 us (33%)
  Pallas kernels  24.7 us (6%)
  other arithmetic  16.3 us (4%)
  local copies, waits for them, and re-layouts  8.59 us (2%)
    ppermute x6, waiting for transfers between devices, hop(): return lax.ppermute(value, 'section', [(source, target)])  122 us
    ppermute x28, starting transfers between devices, z_shift(): return lax.ppermute(value, ('section', 'z'), pairs)  73.6 us
    ppermute x28, waiting for transfers between devices, z_shift(): return lax.ppermute(value, ('section', 'z'), pairs)  69.6 us
    ppermute x25, starting transfers between devices, y_swap(): return lax.ppermute(value, ('section', 'yhi', 'ylo'), pairs)  33.3 us
    pallas_call x6, Pallas kernels, run_block(): pl.pallas_call(functools.partial(block_kernel, seqs, halves, cross, causa...  21.6 us
    ppermute x25, waiting for transfers between devices, y_swap(): return lax.ppermute(value, ('section', 'yhi', 'ylo'), pairs)  21.5 us
    ppermute x14, starting transfers between devices, core_swap(): return lax.ppermute(value, ('section', 'core'), pairs)  19.4 us
  transfers between devices with their start and end apart: 73, of which 26 were waited for; matrix products, arithmetic and copies ran while one was open for 5% of the time, Pallas kernels for 6%

profile of v1, /device:TPU:6, one launch (start us, length us, event | category | flops | bytes accessed | tf_op | source)
XLA Modules:
  0.0 396.4 jit_solution(16686309860954936849)
XLA Ops:
  2.6 3.3 collective-permute-start.12
  17.9 5.9 %collective-permute-start.16 = (bf16[256,1024]{1,0:T(8,128)(2,1)S(1)}, bf16[256,1024]{1,0:T(8,128)(2,1)}, u32[]{:S(2)}, u32[]{:S(2)}) collective-permute-start(bf16[256,1024]{1,0:T(8,128)(2,1)S(1)} %collective-permute-done.12.rest_13_), channel_id=1, source_target_pairs={{0,28},{4,0},{8,4},{12,8},{16,12},{20,16},{24,20},{28,24},{64,92},... | collective-permute-start | bytes 1572872 | tf_op jit(solution)/shard_map/ppermute | solution.py:23
  31.3 4.7 %collective-permute-done.16.rest_20_ = bf16[256,1024]{1,0:T(8,128)(2,1)} collective-permute-done((bf16[256,1024]{1,0:T(8,128)(2,1)S(1)}, bf16[256,1024]{1,0:T(8,128)(2,1)}, u32[]{:S(2)}, u32[]{:S(2)}) %collective-permute-start.16) | collective-permute-done | bytes 524320 | tf_op jit(solution)/shard_map/ppermute | solution.py:23
  36.1 3.8 collective-permute-start.17
  40.8 6.5 %collective-permute-done.9.rest_12_ = bf16[256,1024]{1,0:T(8,128)(2,1)S(1)} collective-permute-done((bf16[256,1024]{1,0:T(8,128)(2,1)S(1)}, bf16[256,1024]{1,0:T(8,128)(2,1)S(1)}, u32[]{:S(2)}, u32[]{:S(2)}) %collective-permute-start.9) | collective-permute-done | bytes 524320 | tf_op jit(solution)/shard_map/ppermute | solution.py:23
  47.3 3.7 collective-permute-start.10
  52.5 5.0 %collective-permute-done.6.rest_7_ = bf16[256,1024]{1,0:T(8,128)(2,1)S(1)} collective-permute-done((bf16[256,1024]{1,0:T(8,128)(2,1)S(1)}, bf16[256,1024]{1,0:T(8,128)(2,1)S(1)}, u32[]{:S(2)}, u32[]{:S(2)}) %collective-permute-start.6) | collective-permute-done | bytes 524320 | tf_op jit(solution)/shard_map/ppermute | solution.py:23
  58.6 3.7 collective-permute-start.18
  66.1 3.7 collective-permute-done.10.rest_11_
  71.4 3.9 collective-permute-start.11
  75.3 4.4 %collective-permute-done.7.rest_8_ = bf16[256,1024]{1,0:T(8,128)(2,1)} collective-permute-done((bf16[256,1024]{1,0:T(8,128)(2,1)S(1)}, bf16[256,1024]{1,0:T(8,128)(2,1)}, u32[]{:S(2)}, u32[]{:S(2)}) %collective-permute-start.7) | collective-permute-done | bytes 524320 | tf_op jit(solution)/shard_map/ppermute | solution.py:23
  81.1 3.7 collective-permute-start.19
  92.3 7.6 %collective-permute-done.8.rest_9_ = bf16[256,1024]{1,0:T(8,128)(2,1)} collective-permute-done((bf16[256,1024]{1,0:T(8,128)(2,1)}, bf16[256,1024]{1,0:T(8,128)(2,1)}, u32[]{:S(2)}, u32[]{:S(2)}) %collective-permute-start.8) | collective-permute-done | bytes 524320 | tf_op jit(solution)/shard_map/ppermute | solution.py:23
  107.6 5.6 %collective-permute-start.34 = (bf16[256,1024]{1,0:T(8,128)(2,1)S(1)}, bf16[256,1024]{1,0:T(8,128)(2,1)S(1)}, u32[]{:S(2)}, u32[]{:S(2)}) collective-permute-start(bf16[256,1024]{1,0:T(8,128)(2,1)S(1)} %copy-done.6), channel_id=1, source_target_pairs={{128,156},{132,128},{136,132},{140,136},{144,140},{148,144},{152,1... | collective-permute-start | bytes 1572872 | tf_op jit(solution)/shard_map/ppermute | solution.py:23
  116.3 5.1 %collective-permute-start.37 = (bf16[256,1024]{1,0:T(8,128)(2,1)S(1)}, bf16[256,1024]{1,0:T(8,128)(2,1)S(1)}, u32[]{:S(2)}, u32[]{:S(2)}) collective-permute-start(bf16[256,1024]{1,0:T(8,128)(2,1)S(1)} %get-tuple-element.19.rest_5_), channel_id=1, source_target_pairs={{128,160},{130,162},{160,128},{162,130},{192,224},{194,226},{224,1... | collective-permute-start | bytes 1572872 | tf_op jit(solution)/shard_map/ppermute | solution.py:28
  127.0 4.4 %collective-permute-done.37.rest_29_ = bf16[256,1024]{1,0:T(8,128)(2,1)S(1)} collective-permute-done((bf16[256,1024]{1,0:T(8,128)(2,1)S(1)}, bf16[256,1024]{1,0:T(8,128)(2,1)S(1)}, u32[]{:S(2)}, u32[]{:S(2)}) %collective-permute-start.37) | collective-permute-done | bytes 524320 | tf_op jit(solution)/shard_map/ppermute | solution.py:28
  144.2 3.6 collective-permute-start.38
  147.9 7.5 %collective-permute-done.41.rest_36_ = bf16[256,1024]{1,0:T(8,128)(2,1)S(1)} collective-permute-done((bf16[256,1024]{1,0:T(8,128)(2,1)S(1)}, bf16[256,1024]{1,0:T(8,128)(2,1)S(1)}, u32[]{:S(2)}, u32[]{:S(2)}) %collective-permute-start.41) | collective-permute-done | bytes 524320 | tf_op jit(solution)/shard_map/ppermute | solution.py:23
  155.3 3.7 collective-permute-start.42
  162.8 3.9 collective-permute-start.32
  172.0 4.9 %collective-permute-start.43 = (bf16[256,1024]{1,0:T(8,128)(2,1)S(1)}, bf16[256,1024]{1,0:T(8,128)(2,1)}, u32[]{:S(2)}, u32[]{:S(2)}) collective-permute-start(bf16[256,1024]{1,0:T(8,128)(2,1)S(1)} %collective-permute-done.42.rest_35_), channel_id=1, source_target_pairs={{128,156},{132,128},{136,132},{140,136},{144,140},{148,144},{152,1... | collective-permute-start | bytes 1572872 | tf_op jit(solution)/shard_map/ppermute | solution.py:23
  179.7 3.6 collective-permute-done.36.rest_26_
  186.8 5.2 %collective-permute-done.39.rest_31_ = bf16[256,1024]{1,0:T(8,128)(2,1)} collective-permute-done((bf16[256,1024]{1,0:T(8,128)(2,1)S(1)}, bf16[256,1024]{1,0:T(8,128)(2,1)}, u32[]{:S(2)}, u32[]{:S(2)}) %collective-permute-start.39) | collective-permute-done | bytes 524320 | tf_op jit(solution)/shard_map/ppermute | solution.py:23
  194.7 4.3 %collective-permute-start.44 = (bf16[256,1024]{1,0:T(8,128)(2,1)}, bf16[256,1024]{1,0:T(8,128)(2,1)}, u32[]{:S(2)}, u32[]{:S(2)}) collective-permute-start(bf16[256,1024]{1,0:T(8,128)(2,1)} %collective-permute-done.43.rest_34_), channel_id=1, source_target_pairs={{128,156},{132,128},{136,132},{140,136},{144,140},{148,144},{152,1... | collective-permute-start | bytes 1572872 | tf_op jit(solution)/shard_map/ppermute | solution.py:23
  199.2 4.0 %collective-permute-done.33.rest_25_ = bf16[256,1024]{1,0:T(8,128)(2,1)} collective-permute-done((bf16[256,1024]{1,0:T(8,128)(2,1)}, bf16[256,1024]{1,0:T(8,128)(2,1)}, u32[]{:S(2)}, u32[]{:S(2)}) %collective-permute-start.33) | collective-permute-done | bytes 524320 | tf_op jit(solution)/shard_map/ppermute | solution.py:23
  203.3 7.6 %collective-permute-done.40.rest_32_ = bf16[256,1024]{1,0:T(8,128)(2,1)} collective-permute-done((bf16[256,1024]{1,0:T(8,128)(2,1)}, bf16[256,1024]{1,0:T(8,128)(2,1)}, u32[]{:S(2)}, u32[]{:S(2)}) %collective-permute-start.40) | collective-permute-done | bytes 524320 | tf_op jit(solution)/shard_map/ppermute | solution.py:23
  219.2 119.0 %collective-permute-done.47 = bf16[128,1024]{1,0:T(8,128)(2,1)S(1)} collective-permute-done((bf16[128,1024]{1,0:T(8,128)(2,1)S(1)}, bf16[128,1024]{1,0:T(8,128)(2,1)S(1)}, u32[]{:S(2)}, u32[]{:S(2)}) %collective-permute-start.47) | collective-permute-done | bytes 262176 | tf_op jit(solution)/shard_map/ppermute | solution.py:37
  348.5 4.1 %collective-permute-done.69 = bf16[128,1024]{1,0:T(8,128)(2,1)S(1)} collective-permute-done((bf16[128,1024]{1,0:T(8,128)(2,1)S(1)}, bf16[128,1024]{1,0:T(8,128)(2,1)S(1)}, u32[]{:S(2)}, u32[]{:S(2)}) %collective-permute-start.69) | collective-permute-done | bytes 262176 | tf_op jit(solution)/shard_map/ppermute | solution.py:28
  354.5 9.0 %shard_map.112 = (bf16[2,128,1024]{2,1,0:T(8,128)(2,1)S(1)}, bf16[2,128,1024]{2,1,0:T(8,128)(2,1)S(1)}) custom-call(s32[44]{0:T(128)S(1)} %concatenate.150.meta, f32[4,1024]{1,0:T(4,128)S(1)} %reshape.595.gain_ref.rest_0_.rest_1_, f32[4,1024]{1,0:T(4,128)S(1)} %reshape.595.gain_ref.rest_0_.rest_1_, f32[8,256]{1,0:T(8,128)S(1)} %select_select_fusion.rest_2_, ...), custom_call_target="tpu_custom_call" | custom-call | flops 2147483648 | bytes 20971520 | tf_op jit(solution)/shard_map/pallas_call | solution.py:230
  366.1 9.0 %shard_map.116 = (bf16[2,128,1024]{2,1,0:T(8,128)(2,1)S(1)}, bf16[2,128,1024]{2,1,0:T(8,128)(2,1)S(1)}) custom-call(s32[44]{0:T(128)S(1)} %concatenate.150.meta, f32[4,1024]{1,0:T(4,128)S(1)} %reshape.595.gain_ref.rest_0_.rest_1_, f32[4,1024]{1,0:T(4,128)S(1)} %reshape.595.gain_ref.rest_0_.rest_1_, f32[8,256]{1,0:T(8,128)S(1)} %select_select_fusion.rest_2_, ...), custom_call_target="tpu_custom_call" | custom-call | flops 2147483648 | bytes 20971520 | tf_op jit(solution)/shard_map/pallas_call | solution.py:230
  384.9 4.9 %collective-permute-done.51 = bf16[128,1024]{1,0:T(8,128)(2,1)S(1)} collective-permute-done((bf16[128,1024]{1,0:T(8,128)(2,1)S(1)}, bf16[128,1024]{1,0:T(8,128)(2,1)S(1)}, u32[]{:S(2)}, u32[]{:S(2)}) %collective-permute-start.51) | collective-permute-done | bytes 262176 | tf_op jit(solution)/shard_map/ppermute | solution.py:28
  389.8 5.1 %collective-permute-done.72 = bf16[128,1024]{1,0:T(8,128)(2,1)S(1)} collective-permute-done((bf16[128,1024]{1,0:T(8,128)(2,1)S(1)}, bf16[128,1024]{1,0:T(8,128)(2,1)S(1)}, u32[]{:S(2)}, u32[]{:S(2)}) %collective-permute-start.72) | collective-permute-done | bytes 262176 | tf_op jit(solution)/shard_map/ppermute | solution.py:28
  (287 shorter events, 120.3 us)
Async XLA Ops:
  13.1 18.2 %collective-permute-start.5 = (bf16[256,1024]{1,0:T(8,128)(2,1)S(1)}, bf16[256,1024]{1,0:T(8,128)(2,1)S(1)}, u32[]{:S(2)}, u32[]{:S(2)}) collective-permute-start(bf16[256,1024]{1,0:T(8,128)(2,1)S(1)} %get-tuple-element.19.rest_5_), channel_id=1, source_target_pairs={{0,4},{4,8},{8,12},{12,16},{16,20},{20,24},{24,28},{28,0},{64,68},... | collective-permute-start | bytes 1572872 | tf_op jit(solution)/shard_map/ppermute | solution.py:23
  17.9 18.2 %collective-permute-start.16 = (bf16[256,1024]{1,0:T(8,128)(2,1)S(1)}, bf16[256,1024]{1,0:T(8,128)(2,1)}, u32[]{:S(2)}, u32[]{:S(2)}) collective-permute-start(bf16[256,1024]{1,0:T(8,128)(2,1)S(1)} %collective-permute-done.12.rest_13_), channel_id=1, source_target_pairs={{0,28},{4,0},{8,4},{12,8},{16,12},{20,16},{24,20},{28,24},{64,92},... | collective-permute-start | bytes 1572872 | tf_op jit(solution)/shard_map/ppermute | solution.py:23
  25.2 22.1 %collective-permute-start.9 = (bf16[256,1024]{1,0:T(8,128)(2,1)S(1)}, bf16[256,1024]{1,0:T(8,128)(2,1)S(1)}, u32[]{:S(2)}, u32[]{:S(2)}) collective-permute-start(bf16[256,1024]{1,0:T(8,128)(2,1)S(1)} %get-tuple-element.19.rest_5_), channel_id=1, source_target_pairs={{0,28},{4,0},{8,4},{12,8},{16,12},{20,16},{24,20},{28,24},{64,92},... | collective-permute-start | bytes 1572872 | tf_op jit(solution)/shard_map/ppermute | solution.py:23
  28.5 42.9 %collective-permute-start.4 = (bf16[4,128,1024]{2,1,0:T(8,128)(2,1)}, bf16[4,128,1024]{2,1,0:T(8,128)(2,1)}, u32[]{:S(2)}, u32[]{:S(2)}) collective-permute-start(bf16[4,128,1024]{2,1,0:T(8,128)(2,1)} %pad_maximum_fusion.first), channel_id=1, source_target_pairs={{0,1},{1,0},{64,65},{65,64},{2,3},{3,2},{66,67},{67,66},{4,5},{5,4... | collective-permute-start | bytes 3145736 | tf_op jit(solution)/shard_map/ppermute | solution.py:33
  30.1 22.2 %collective-permute-start.13 = (bf16[256,1024]{1,0:T(8,128)(2,1)S(1)}, bf16[256,1024]{1,0:T(8,128)(2,1)S(1)}, u32[]{:S(2)}, u32[]{:S(2)}) collective-permute-start(bf16[256,1024]{1,0:T(8,128)(2,1)S(1)} %collective-permute-done.12.rest_13_), channel_id=1, source_target_pairs={{0,4},{4,8},{8,12},{12,16},{16,20},{20,24},{24,28},{28,0},{64,68},... | collective-permute-start | bytes 1572872 | tf_op jit(solution)/shard_map/ppermute | solution.py:23
  31.2 26.2 %collective-permute-start.6 = (bf16[256,1024]{1,0:T(8,128)(2,1)S(1)}, bf16[256,1024]{1,0:T(8,128)(2,1)S(1)}, u32[]{:S(2)}, u32[]{:S(2)}) collective-permute-start(bf16[256,1024]{1,0:T(8,128)(2,1)S(1)} %collective-permute-done.5.rest_6_), channel_id=1, source_target_pairs={{0,4},{4,8},{8,12},{12,16},{16,20},{20,24},{24,28},{28,0},{64,68},... | collective-permute-start | bytes 1572872 | tf_op jit(solution)/shard_map/ppermute | solution.py:23
  36.1 22.6 %collective-permute-start.17 = (bf16[256,1024]{1,0:T(8,128)(2,1)}, bf16[256,1024]{1,0:T(8,128)(2,1)}, u32[]{:S(2)}, u32[]{:S(2)}) collective-permute-start(bf16[256,1024]{1,0:T(8,128)(2,1)} %collective-permute-done.16.rest_20_), channel_id=1, source_target_pairs={{0,28},{4,0},{8,4},{12,8},{16,12},{20,16},{24,20},{28,24},{64,92},... | collective-permute-start | bytes 1572872 | tf_op jit(solution)/shard_map/ppermute | solution.py:23
  47.3 22.5 %collective-permute-start.10 = (bf16[256,1024]{1,0:T(8,128)(2,1)S(1)}, bf16[256,1024]{1,0:T(8,128)(2,1)}, u32[]{:S(2)}, u32[]{:S(2)}) collective-permute-start(bf16[256,1024]{1,0:T(8,128)(2,1)S(1)} %collective-permute-done.9.rest_12_), channel_id=1, source_target_pairs={{0,28},{4,0},{8,4},{12,8},{16,12},{20,16},{24,20},{28,24},{64,92},... | collective-permute-start | bytes 1572872 | tf_op jit(solution)/shard_map/ppermute | solution.py:23
  52.4 23.0 %collective-permute-start.14 = (bf16[256,1024]{1,0:T(8,128)(2,1)S(1)}, bf16[256,1024]{1,0:T(8,128)(2,1)}, u32[]{:S(2)}, u32[]{:S(2)}) collective-permute-start(bf16[256,1024]{1,0:T(8,128)(2,1)S(1)} %collective-permute-done.13.rest_14_), channel_id=1, source_target_pairs={{0,4},{4,8},{8,12},{12,16},{16,20},{20,24},{24,28},{28,0},{64,68},... | collective-permute-start | bytes 1572872 | tf_op jit(solution)/shard_map/ppermute | solution.py:23
  57.5 22.2 %collective-permute-start.7 = (bf16[256,1024]{1,0:T(8,128)(2,1)S(1)}, bf16[256,1024]{1,0:T(8,128)(2,1)}, u32[]{:S(2)}, u32[]{:S(2)}) collective-permute-start(bf16[256,1024]{1,0:T(8,128)(2,1)S(1)} %collective-permute-done.6.rest_7_), channel_id=1, source_target_pairs={{0,4},{4,8},{8,12},{12,16},{16,20},{20,24},{24,28},{28,0},{64,68},... | collective-permute-start | bytes 1572872 | tf_op jit(solution)/shard_map/ppermute | solution.py:23
  58.6 22.5 %collective-permute-start.18 = (bf16[256,1024]{1,0:T(8,128)(2,1)}, bf16[256,1024]{1,0:T(8,128)(2,1)}, u32[]{:S(2)}, u32[]{:S(2)}) collective-permute-start(bf16[256,1024]{1,0:T(8,128)(2,1)} %collective-permute-done.17.rest_19_), channel_id=1, source_target_pairs={{0,28},{4,0},{8,4},{12,8},{16,12},{20,16},{24,20},{28,24},{64,92},... | collective-permute-start | bytes 1572872 | tf_op jit(solution)/shard_map/ppermute | solution.py:23
  69.8 33.3 %collective-permute-start.55 = (bf16[4,128,1024]{2,1,0:T(8,128)(2,1)}, bf16[4,128,1024]{2,1,0:T(8,128)(2,1)}, u32[]{:S(2)}, u32[]{:S(2)}) collective-permute-start(bf16[4,128,1024]{2,1,0:T(8,128)(2,1)} %pad_maximum_fusion.2.first), channel_id=1, source_target_pairs={{0,1},{1,0},{64,65},{65,64},{2,3},{3,2},{66,67},{67,66},{4,5},{5,4... | collective-permute-start | bytes 3145736 | tf_op jit(solution)/shard_map/ppermute | solution.py:33
  71.4 20.9 %collective-permute-start.11 = (bf16[256,1024]{1,0:T(8,128)(2,1)}, bf16[256,1024]{1,0:T(8,128)(2,1)}, u32[]{:S(2)}, u32[]{:S(2)}) collective-permute-start(bf16[256,1024]{1,0:T(8,128)(2,1)} %collective-permute-done.10.rest_11_), channel_id=1, source_target_pairs={{0,28},{4,0},{8,4},{12,8},{16,12},{20,16},{24,20},{28,24},{64,92},... | collective-permute-start | bytes 1572872 | tf_op jit(solution)/shard_map/ppermute | solution.py:23
  75.3 17.0 %collective-permute-start.15 = (bf16[256,1024]{1,0:T(8,128)(2,1)}, bf16[256,1024]{1,0:T(8,128)(2,1)}, u32[]{:S(2)}, u32[]{:S(2)}) collective-permute-start(bf16[256,1024]{1,0:T(8,128)(2,1)} %collective-permute-done.14.rest_15_), channel_id=1, source_target_pairs={{0,4},{4,8},{8,12},{12,16},{16,20},{20,24},{24,28},{28,0},{64,68},... | collective-permute-start | bytes 1572872 | tf_op jit(solution)/shard_map/ppermute | solution.py:23
  79.7 20.3 %collective-permute-start.8 = (bf16[256,1024]{1,0:T(8,128)(2,1)}, bf16[256,1024]{1,0:T(8,128)(2,1)}, u32[]{:S(2)}, u32[]{:S(2)}) collective-permute-start(bf16[256,1024]{1,0:T(8,128)(2,1)} %collective-permute-done.7.rest_8_), channel_id=1, source_target_pairs={{0,4},{4,8},{8,12},{12,16},{16,20},{20,24},{24,28},{28,0},{64,68},... | collective-permute-start | bytes 1572872 | tf_op jit(solution)/shard_map/ppermute | solution.py:23
  81.1 20.5 %collective-permute-start.19 = (bf16[256,1024]{1,0:T(8,128)(2,1)}, bf16[256,1024]{1,0:T(8,128)(2,1)}, u32[]{:S(2)}, u32[]{:S(2)}) collective-permute-start(bf16[256,1024]{1,0:T(8,128)(2,1)} %collective-permute-done.18.rest_18_), channel_id=1, source_target_pairs={{0,28},{4,0},{8,4},{12,8},{16,12},{20,16},{24,20},{28,24},{64,92},... | collective-permute-start | bytes 1572872 | tf_op jit(solution)/shard_map/ppermute | solution.py:23
  131.4 27.6 %collective-permute-start.35 = (bf16[256,1024]{1,0:T(8,128)(2,1)S(1)}, bf16[256,1024]{1,0:T(8,128)(2,1)S(1)}, u32[]{:S(2)}, u32[]{:S(2)}) collective-permute-start(bf16[256,1024]{1,0:T(8,128)(2,1)S(1)} %collective-permute-done.34.rest_28_), channel_id=1, source_target_pairs={{128,156},{132,128},{136,132},{140,136},{144,140},{148,144},{152,1... | collective-permute-start | bytes 1572872 | tf_op jit(solution)/shard_map/ppermute | solution.py:23
  133.6 21.7 %collective-permute-start.41 = (bf16[256,1024]{1,0:T(8,128)(2,1)S(1)}, bf16[256,1024]{1,0:T(8,128)(2,1)S(1)}, u32[]{:S(2)}, u32[]{:S(2)}) collective-permute-start(bf16[256,1024]{1,0:T(8,128)(2,1)S(1)} %collective-permute-done.37.rest_29_), channel_id=1, source_target_pairs={{128,156},{132,128},{136,132},{140,136},{144,140},{148,144},{152,1... | collective-permute-start | bytes 1572872 | tf_op jit(solution)/shard_map/ppermute | solution.py:23
  139.7 20.0 %collective-permute-start.28 = (bf16[2,128,1024]{2,1,0:T(8,128)(2,1)S(1)}, bf16[2,128,1024]{2,1,0:T(8,128)(2,1)S(1)}, u32[]{:S(2)}, u32[]{:S(2)}) collective-permute-start(bf16[2,128,1024]{2,1,0:T(8,128)(2,1)S(1)} %get-tuple-element.82), channel_id=1, source_target_pairs={{128,130},{130,128},{160,162},{162,160},{129,131},{131,129},{161,1... | collective-permute-start | bytes 1572872 | tf_op jit(solution)/shard_map/ppermute | solution.py:28
  141.2 21.6 %collective-permute-start.31 = (bf16[256,1024]{1,0:T(8,128)(2,1)S(1)}, bf16[256,1024]{1,0:T(8,128)(2,1)S(1)}, u32[]{:S(2)}, u32[]{:S(2)}) collective-permute-start(bf16[256,1024]{1,0:T(8,128)(2,1)S(1)} %collective-permute-done.30.rest_22_), channel_id=1, source_target_pairs={{128,132},{132,136},{136,140},{140,144},{144,148},{148,152},{152,1... | collective-permute-start | bytes 1572872 | tf_op jit(solution)/shard_map/ppermute | solution.py:23
  144.2 22.7 %collective-permute-start.38 = (bf16[256,1024]{1,0:T(8,128)(2,1)S(1)}, bf16[256,1024]{1,0:T(8,128)(2,1)S(1)}, u32[]{:S(2)}, u32[]{:S(2)}) collective-permute-start(bf16[256,1024]{1,0:T(8,128)(2,1)S(1)} %collective-permute-done.37.rest_29_), channel_id=1, source_target_pairs={{128,132},{132,136},{136,140},{140,144},{144,148},{148,152},{152,1... | collective-permute-start | bytes 1572872 | tf_op jit(solution)/shard_map/ppermute | solution.py:23
  159.0 17.9 %collective-permute-start.64 = (bf16[2,128,1024]{2,1,0:T(8,128)(2,1)S(1)}, bf16[2,128,1024]{2,1,0:T(8,128)(2,1)S(1)}, u32[]{:S(2)}, u32[]{:S(2)}) collective-permute-start(bf16[2,128,1024]{2,1,0:T(8,128)(2,1)S(1)} %get-tuple-element.84), channel_id=1, source_target_pairs={{128,130},{130,128},{160,162},{162,160},{129,131},{131,129},{161,1... | collective-permute-start | bytes 1572872 | tf_op jit(solution)/shard_map/ppermute | solution.py:28
  159.8 23.5 %collective-permute-start.36 = (bf16[256,1024]{1,0:T(8,128)(2,1)S(1)}, bf16[256,1024]{1,0:T(8,128)(2,1)S(1)}, u32[]{:S(2)}, u32[]{:S(2)}) collective-permute-start(bf16[256,1024]{1,0:T(8,128)(2,1)S(1)} %collective-permute-done.35.rest_27_), channel_id=1, source_target_pairs={{128,156},{132,128},{136,132},{140,136},{144,140},{148,144},{152,1... | collective-permute-start | bytes 1572872 | tf_op jit(solution)/shard_map/ppermute | solution.py:23
  162.8 22.1 %collective-permute-start.32 = (bf16[256,1024]{1,0:T(8,128)(2,1)S(1)}, bf16[256,1024]{1,0:T(8,128)(2,1)}, u32[]{:S(2)}, u32[]{:S(2)}) collective-permute-start(bf16[256,1024]{1,0:T(8,128)(2,1)S(1)} %collective-permute-done.31.rest_23_), channel_id=1, source_target_pairs={{128,132},{132,136},{136,140},{140,144},{144,148},{148,152},{152,1... | collective-permute-start | bytes 1572872 | tf_op jit(solution)/shard_map/ppermute | solution.py:23
  166.9 25.1 %collective-permute-start.39 = (bf16[256,1024]{1,0:T(8,128)(2,1)S(1)}, bf16[256,1024]{1,0:T(8,128)(2,1)}, u32[]{:S(2)}, u32[]{:S(2)}) collective-permute-start(bf16[256,1024]{1,0:T(8,128)(2,1)S(1)} %collective-permute-done.38.rest_30_), channel_id=1, source_target_pairs={{128,132},{132,136},{136,140},{140,144},{144,148},{148,152},{152,1... | collective-permute-start | bytes 1572872 | tf_op jit(solution)/shard_map/ppermute | solution.py:23
  172.0 22.7 %collective-permute-start.43 = (bf16[256,1024]{1,0:T(8,128)(2,1)S(1)}, bf16[256,1024]{1,0:T(8,128)(2,1)}, u32[]{:S(2)}, u32[]{:S(2)}) collective-permute-start(bf16[256,1024]{1,0:T(8,128)(2,1)S(1)} %collective-permute-done.42.rest_35_), channel_id=1, source_target_pairs={{128,156},{132,128},{136,132},{140,136},{144,140},{148,144},{152,1... | collective-permute-start | bytes 1572872 | tf_op jit(solution)/shard_map/ppermute | solution.py:23
  176.9 33.9 %collective-permute-start.29 = (bf16[2,2,128,1024]{3,2,1,0:T(8,128)(2,1)}, bf16[2,2,128,1024]{3,2,1,0:T(8,128)(2,1)}, u32[]{:S(2)}, u32[]{:S(2)}) collective-permute-start(bf16[2,2,128,1024]{3,2,1,0:T(8,128)(2,1)} %pad_maximum_fusion.1.rest_3_), channel_id=1, source_target_pairs={{128,129},{129,128},{130,131},{131,130},{132,133},{133,132},{134,1... | collective-permute-start | bytes 3145736 | tf_op jit(solution)/shard_map/ppermute | solution.py:33
  183.3 29.6 %collective-permute-start.65 = (bf16[2,2,128,1024]{3,2,1,0:T(8,128)(2,1)}, bf16[2,2,128,1024]{3,2,1,0:T(8,128)(2,1)}, u32[]{:S(2)}, u32[]{:S(2)}) collective-permute-start(bf16[2,2,128,1024]{3,2,1,0:T(8,128)(2,1)} %pad_maximum_fusion.3.rest_3_), channel_id=1, source_target_pairs={{128,129},{129,128},{130,131},{131,130},{132,133},{133,132},{134,1... | collective-permute-start | bytes 3145736 | tf_op jit(solution)/shard_map/ppermute | solution.py:33
  184.9 18.3 %collective-permute-start.33 = (bf16[256,1024]{1,0:T(8,128)(2,1)}, bf16[256,1024]{1,0:T(8,128)(2,1)}, u32[]{:S(2)}, u32[]{:S(2)}) collective-permute-start(bf16[256,1024]{1,0:T(8,128)(2,1)} %collective-permute-done.32.rest_24_), channel_id=1, source_target_pairs={{128,132},{132,136},{136,140},{140,144},{144,148},{148,152},{152,1... | collective-permute-start | bytes 1572872 | tf_op jit(solution)/shard_map/ppermute | solution.py:23
  192.0 18.8 %collective-permute-start.40 = (bf16[256,1024]{1,0:T(8,128)(2,1)}, bf16[256,1024]{1,0:T(8,128)(2,1)}, u32[]{:S(2)}, u32[]{:S(2)}) collective-permute-start(bf16[256,1024]{1,0:T(8,128)(2,1)} %collective-permute-done.39.rest_31_), channel_id=1, source_target_pairs={{128,132},{132,136},{136,140},{140,144},{144,148},{148,152},{152,1... | collective-permute-start | bytes 1572872 | tf_op jit(solution)/shard_map/ppermute | solution.py:23
  216.4 121.8 %collective-permute-start.47 = (bf16[128,1024]{1,0:T(8,128)(2,1)S(1)}, bf16[128,1024]{1,0:T(8,128)(2,1)S(1)}, u32[]{:S(2)}, u32[]{:S(2)}) collective-permute-start(bf16[128,1024]{1,0:T(8,128)(2,1)S(1)} %fusion.15), channel_id=1, source_target_pairs={{128,192},{129,193},{130,194},{131,195},{132,196},{133,197},{134,1... | collective-permute-start | bytes 786440 | tf_op jit(solution)/shard_map/ppermute | solution.py:37
  217.9 126.0 %collective-permute-start.68 = (bf16[128,1024]{1,0:T(8,128)(2,1)S(1)}, bf16[128,1024]{1,0:T(8,128)(2,1)S(1)}, u32[]{:S(2)}, u32[]{:S(2)}) collective-permute-start(bf16[128,1024]{1,0:T(8,128)(2,1)S(1)} %fusion.7), channel_id=1, source_target_pairs={{128,192},{129,193},{130,194},{131,195},{132,196},{133,197},{134,1... | collective-permute-start | bytes 786440 | tf_op jit(solution)/shard_map/ppermute | solution.py:37
  (95 other events, 1732.8 us)

commit v2 on v1

--- a/solution.py
+++ b/solution.py
@@ -301,8 +301,10 @@
     near_list = ring(own, 4, 3, everywhere)
     cross_list = ring(crossed, 3, 4, everywhere)
     half_one = near_list + cross_list
-    far_own = ring(other, 4, 3, (2, 3))
-    far_cross = ring(y_swap(own, 2, (2, 3)), 3, 4, (2, 3))
+    far_own = ring(other, 5, 2, (2, 3))
+    far_left = ring(y_swap(own, 2, (2, 3)), 0, 4, (2, 3))
+    far_near = [y_swap(near_list[k], 2, (2, 3)) for k in (1, 2, 3)]
+    far_cross = far_left[:1] + far_near + far_left[1:]
     half_two = far_own + far_cross
 
     slots = jnp.arange(BLOCKS, dtype=jnp.int32)

time: 398 us -> 391 us (0.982)
  waiting for transfers between devices: 213 us -> 198 us
  starting transfers between devices: 132 us -> 139 us
    ppermute x25 -> x28, starting transfers between devices: 33.3 us -> 46.8 us  [y_swap(): return lax.ppermute(value, ('section', 'yhi', 'ylo'), pairs)]
    ppermute x28 -> x25, waiting for transfers between devices: 69.6 us -> 56.5 us  [z_shift(): return lax.ppermute(value, ('section', 'z'), pairs)]
    ppermute x28 -> x25, starting transfers between devices: 73.6 us -> 67.9 us  [z_shift(): return lax.ppermute(value, ('section', 'z'), pairs)]
    ppermute x25 -> x28, waiting for transfers between devices: 21.5 us -> 21.4 us  [y_swap(): return lax.ppermute(value, ('section', 'yhi', 'ylo'), pairs)]
where the time goes in v2:
time: 391 us; the launch traced here: 389 us
  waiting for transfers between devices  198 us (51%)
  starting transfers between devices  139 us (36%)
  Pallas kernels  24.6 us (6%)
  other arithmetic  16.4 us (4%)
  local copies, waits for them, and re-layouts  8.6 us (2%)
    ppermute x6, waiting for transfers between devices, hop(): return lax.ppermute(value, 'section', [(source, target)])  120 us
    ppermute x25, starting transfers between devices, z_shift(): return lax.ppermute(value, ('section', 'z'), pairs)  67.9 us
    ppermute x25, waiting for transfers between devices, z_shift(): return lax.ppermute(value, ('section', 'z'), pairs)  56.5 us
    ppermute x28, starting transfers between devices, y_swap(): return lax.ppermute(value, ('section', 'yhi', 'ylo'), pairs)  46.8 us
    pallas_call x6, Pallas kernels, run_block(): pl.pallas_call(functools.partial(block_kernel, seqs, halves, cross, causa...  21.5 us
    ppermute x28, waiting for transfers between devices, y_swap(): return lax.ppermute(value, ('section', 'yhi', 'ylo'), pairs)  21.4 us
    ppermute x14, starting transfers between devices, core_swap(): return lax.ppermute(value, ('section', 'core'), pairs)  19.5 us
  transfers between devices with their start and end apart: 73, of which 26 were waited for; matrix products, arithmetic and copies ran while one was open for 5% of the time, Pallas kernels for 6%

profile of v2, /device:TPU:6, one launch (start us, length us, event | category | flops | bytes accessed | tf_op | source)
XLA Modules:
  0.0 389.1 jit_solution(584684887546587435)
XLA Ops:
  2.6 3.3 collective-permute-start.12
  17.9 5.9 %collective-permute-start.16 = (bf16[256,1024]{1,0:T(8,128)(2,1)S(1)}, bf16[256,1024]{1,0:T(8,128)(2,1)}, u32[]{:S(2)}, u32[]{:S(2)}) collective-permute-start(bf16[256,1024]{1,0:T(8,128)(2,1)S(1)} %collective-permute-done.12.rest_13_), channel_id=1, source_target_pairs={{0,28},{4,0},{8,4},{12,8},{16,12},{20,16},{24,20},{28,24},{64,92},... | collective-permute-start | bytes 1572872 | tf_op jit(solution)/shard_map/ppermute | solution.py:23
  31.4 4.7 %collective-permute-done.16.rest_20_ = bf16[256,1024]{1,0:T(8,128)(2,1)} collective-permute-done((bf16[256,1024]{1,0:T(8,128)(2,1)S(1)}, bf16[256,1024]{1,0:T(8,128)(2,1)}, u32[]{:S(2)}, u32[]{:S(2)}) %collective-permute-start.16) | collective-permute-done | bytes 524320 | tf_op jit(solution)/shard_map/ppermute | solution.py:23
  36.1 3.8 collective-permute-start.17
  40.8 6.5 %collective-permute-done.9.rest_12_ = bf16[256,1024]{1,0:T(8,128)(2,1)S(1)} collective-permute-done((bf16[256,1024]{1,0:T(8,128)(2,1)S(1)}, bf16[256,1024]{1,0:T(8,128)(2,1)S(1)}, u32[]{:S(2)}, u32[]{:S(2)}) %collective-permute-start.9) | collective-permute-done | bytes 524320 | tf_op jit(solution)/shard_map/ppermute | solution.py:23
  47.3 3.7 collective-permute-start.10
  52.5 5.0 %collective-permute-done.6.rest_7_ = bf16[256,1024]{1,0:T(8,128)(2,1)S(1)} collective-permute-done((bf16[256,1024]{1,0:T(8,128)(2,1)S(1)}, bf16[256,1024]{1,0:T(8,128)(2,1)S(1)}, u32[]{:S(2)}, u32[]{:S(2)}) %collective-permute-start.6) | collective-permute-done | bytes 524320 | tf_op jit(solution)/shard_map/ppermute | solution.py:23
  58.6 3.7 collective-permute-start.18
  66.1 3.7 collective-permute-done.10.rest_11_
  71.4 3.9 collective-permute-start.11
  75.3 4.4 %collective-permute-done.7.rest_8_ = bf16[256,1024]{1,0:T(8,128)(2,1)} collective-permute-done((bf16[256,1024]{1,0:T(8,128)(2,1)S(1)}, bf16[256,1024]{1,0:T(8,128)(2,1)}, u32[]{:S(2)}, u32[]{:S(2)}) %collective-permute-start.7) | collective-permute-done | bytes 524320 | tf_op jit(solution)/shard_map/ppermute | solution.py:23
  81.1 3.7 collective-permute-start.19
  92.3 7.6 %collective-permute-done.8.rest_9_ = bf16[256,1024]{1,0:T(8,128)(2,1)} collective-permute-done((bf16[256,1024]{1,0:T(8,128)(2,1)}, bf16[256,1024]{1,0:T(8,128)(2,1)}, u32[]{:S(2)}, u32[]{:S(2)}) %collective-permute-start.8) | collective-permute-done | bytes 524320 | tf_op jit(solution)/shard_map/ppermute | solution.py:23
  112.7 5.1 %collective-permute-start.37 = (bf16[256,1024]{1,0:T(8,128)(2,1)S(1)}, bf16[256,1024]{1,0:T(8,128)(2,1)S(1)}, u32[]{:S(2)}, u32[]{:S(2)}) collective-permute-start(bf16[256,1024]{1,0:T(8,128)(2,1)S(1)} %get-tuple-element.19.rest_5_), channel_id=1, source_target_pairs={{128,160},{130,162},{160,128},{162,130},{192,224},{194,226},{224,1... | collective-permute-start | bytes 1572872 | tf_op jit(solution)/shard_map/ppermute | solution.py:28
  118.1 5.3 %collective-permute-done.30.rest_22_ = bf16[256,1024]{1,0:T(8,128)(2,1)S(1)} collective-permute-done((bf16[256,1024]{1,0:T(8,128)(2,1)S(1)}, bf16[256,1024]{1,0:T(8,128)(2,1)S(1)}, u32[]{:S(2)}, u32[]{:S(2)}) %collective-permute-start.30) | collective-permute-done | bytes 524320 | tf_op jit(solution)/shard_map/ppermute | solution.py:23
  123.4 3.6 collective-permute-start.35
  131.7 4.9 %collective-permute-start.41 = (bf16[256,1024]{1,0:T(8,128)(2,1)S(1)}, bf16[256,1024]{1,0:T(8,128)(2,1)S(1)}, u32[]{:S(2)}, u32[]{:S(2)}) collective-permute-start(bf16[256,1024]{1,0:T(8,128)(2,1)S(1)} %collective-permute-done.37.rest_29_), channel_id=1, source_target_pairs={{128,156},{132,128},{136,132},{140,136},{144,140},{148,144},{152,1... | collective-permute-start | bytes 1572872 | tf_op jit(solution)/shard_map/ppermute | solution.py:23
  144.1 3.9 collective-permute-done.41.rest_36_
  147.9 4.6 %collective-permute-start.36 = (bf16[256,1024]{1,0:T(8,128)(2,1)S(1)}, bf16[256,1024]{1,0:T(8,128)(2,1)S(1)}, u32[]{:S(2)}, u32[]{:S(2)}) collective-permute-start(bf16[256,1024]{1,0:T(8,128)(2,1)S(1)} %collective-permute-done.35.rest_28_), channel_id=1, source_target_pairs={{128,156},{132,128},{136,132},{140,136},{144,140},{148,144},{152,1... | collective-permute-start | bytes 1572872 | tf_op jit(solution)/shard_map/ppermute | solution.py:23
  154.5 5.1 %collective-permute-start.42 = (bf16[256,1024]{1,0:T(8,128)(2,1)S(1)}, bf16[256,1024]{1,0:T(8,128)(2,1)S(1)}, u32[]{:S(2)}, u32[]{:S(2)}) collective-permute-start(bf16[256,1024]{1,0:T(8,128)(2,1)S(1)} %collective-permute-done.41.rest_36_), channel_id=1, source_target_pairs={{128,156},{132,128},{136,132},{140,136},{144,140},{148,144},{152,1... | collective-permute-start | bytes 1572872 | tf_op jit(solution)/shard_map/ppermute | solution.py:23
  160.5 5.1 %collective-permute-start.38 = (bf16[256,1024]{1,0:T(8,128)(2,1)S(1)}, bf16[256,1024]{1,0:T(8,128)(2,1)S(1)}, u32[]{:S(2)}, u32[]{:S(2)}) collective-permute-start(bf16[256,1024]{1,0:T(8,128)(2,1)S(1)} %collective-permute-done.5.rest_6_), channel_id=1, source_target_pairs={{128,160},{130,162},{160,128},{162,130},{192,224},{194,226},{224,1... | collective-permute-start | bytes 1572872 | tf_op jit(solution)/shard_map/ppermute | solution.py:28
  172.9 5.6 %collective-permute-start.43 = (bf16[256,1024]{1,0:T(8,128)(2,1)S(1)}, bf16[256,1024]{1,0:T(8,128)(2,1)}, u32[]{:S(2)}, u32[]{:S(2)}) collective-permute-start(bf16[256,1024]{1,0:T(8,128)(2,1)S(1)} %collective-permute-done.42.rest_35_), channel_id=1, source_target_pairs={{128,156},{132,128},{136,132},{140,136},{144,140},{148,144},{152,1... | collective-permute-start | bytes 1572872 | tf_op jit(solution)/shard_map/ppermute | solution.py:23
  185.9 5.1 %collective-permute-start.40 = (bf16[256,1024]{1,0:T(8,128)(2,1)}, bf16[256,1024]{1,0:T(8,128)(2,1)}, u32[]{:S(2)}, u32[]{:S(2)}) collective-permute-start(bf16[256,1024]{1,0:T(8,128)(2,1)} %collective-permute-done.7.rest_8_), channel_id=1, source_target_pairs={{128,160},{130,162},{160,128},{162,130},{192,224},{194,226},{224,1... | collective-permute-start | bytes 1572872 | tf_op jit(solution)/shard_map/ppermute | solution.py:28
  192.9 5.1 %collective-permute-start.44 = (bf16[256,1024]{1,0:T(8,128)(2,1)}, bf16[256,1024]{1,0:T(8,128)(2,1)}, u32[]{:S(2)}, u32[]{:S(2)}) collective-permute-start(bf16[256,1024]{1,0:T(8,128)(2,1)} %collective-permute-done.43.rest_34_), channel_id=1, source_target_pairs={{128,156},{132,128},{136,132},{140,136},{144,140},{148,144},{152,1... | collective-permute-start | bytes 1572872 | tf_op jit(solution)/shard_map/ppermute | solution.py:23
  199.5 4.6 %collective-permute-done.34.rest_26_ = bf16[256,1024]{1,0:T(8,128)(2,1)} collective-permute-done((bf16[256,1024]{1,0:T(8,128)(2,1)}, bf16[256,1024]{1,0:T(8,128)(2,1)}, u32[]{:S(2)}, u32[]{:S(2)}) %collective-permute-start.34) | collective-permute-done | bytes 524320 | tf_op jit(solution)/shard_map/ppermute | solution.py:23
  213.6 117.3 %collective-permute-done.47 = bf16[128,1024]{1,0:T(8,128)(2,1)S(1)} collective-permute-done((bf16[128,1024]{1,0:T(8,128)(2,1)S(1)}, bf16[128,1024]{1,0:T(8,128)(2,1)S(1)}, u32[]{:S(2)}, u32[]{:S(2)}) %collective-permute-start.47) | collective-permute-done | bytes 262176 | tf_op jit(solution)/shard_map/ppermute | solution.py:37
  341.2 4.1 %collective-permute-done.69 = bf16[128,1024]{1,0:T(8,128)(2,1)S(1)} collective-permute-done((bf16[128,1024]{1,0:T(8,128)(2,1)S(1)}, bf16[128,1024]{1,0:T(8,128)(2,1)S(1)}, u32[]{:S(2)}, u32[]{:S(2)}) %collective-permute-start.69) | collective-permute-done | bytes 262176 | tf_op jit(solution)/shard_map/ppermute | solution.py:28
  347.3 9.0 %shard_map.112 = (bf16[2,128,1024]{2,1,0:T(8,128)(2,1)S(1)}, bf16[2,128,1024]{2,1,0:T(8,128)(2,1)S(1)}) custom-call(s32[44]{0:T(128)S(1)} %concatenate.150.meta, f32[4,1024]{1,0:T(4,128)S(1)} %reshape.595.gain_ref.rest_0_.rest_1_, f32[4,1024]{1,0:T(4,128)S(1)} %reshape.595.gain_ref.rest_0_.rest_1_, f32[8,256]{1,0:T(8,128)S(1)} %select_select_fusion.rest_2_, ...), custom_call_target="tpu_custom_call" | custom-call | flops 2147483648 | bytes 20971520 | tf_op jit(solution)/shard_map/pallas_call | solution.py:230
  358.9 9.0 %shard_map.116 = (bf16[2,128,1024]{2,1,0:T(8,128)(2,1)S(1)}, bf16[2,128,1024]{2,1,0:T(8,128)(2,1)S(1)}) custom-call(s32[44]{0:T(128)S(1)} %concatenate.150.meta, f32[4,1024]{1,0:T(4,128)S(1)} %reshape.595.gain_ref.rest_0_.rest_1_, f32[4,1024]{1,0:T(4,128)S(1)} %reshape.595.gain_ref.rest_0_.rest_1_, f32[8,256]{1,0:T(8,128)S(1)} %select_select_fusion.rest_2_, ...), custom_call_target="tpu_custom_call" | custom-call | flops 2147483648 | bytes 20971520 | tf_op jit(solution)/shard_map/pallas_call | solution.py:230
  374.0 3.4 collective-permute-start.72
  377.7 4.9 %collective-permute-done.51 = bf16[128,1024]{1,0:T(8,128)(2,1)S(1)} collective-permute-done((bf16[128,1024]{1,0:T(8,128)(2,1)S(1)}, bf16[128,1024]{1,0:T(8,128)(2,1)S(1)}, u32[]{:S(2)}, u32[]{:S(2)}) %collective-permute-start.51) | collective-permute-done | bytes 262176 | tf_op jit(solution)/shard_map/ppermute | solution.py:28
  382.5 5.1 %collective-permute-done.72 = bf16[128,1024]{1,0:T(8,128)(2,1)S(1)} collective-permute-done((bf16[128,1024]{1,0:T(8,128)(2,1)S(1)}, bf16[128,1024]{1,0:T(8,128)(2,1)S(1)}, u32[]{:S(2)}, u32[]{:S(2)}) %collective-permute-start.72) | collective-permute-done | bytes 262176 | tf_op jit(solution)/shard_map/ppermute | solution.py:28
  (289 shorter events, 116.8 us)
Async XLA Ops:
  7.0 16.7 %collective-permute-start.3 = (bf16[128,1024]{1,0:T(8,128)(2,1)S(1)}, bf16[128,1024]{1,0:T(8,128)(2,1)}, u32[]{:S(2)}, u32[]{:S(2)}) collective-permute-start(bf16[128,1024]{1,0:T(8,128)(2,1)S(1)} %get-tuple-element.76), channel_id=1, source_target_pairs={{0,34},{2,32},{32,2},{34,0},{64,98},{66,96},{96,66},{98,64},{1,35}... | collective-permute-start | bytes 786440 | tf_op jit(solution)/shard_map/ppermute | solution.py:28
  13.1 18.2 %collective-permute-start.5 = (bf16[256,1024]{1,0:T(8,128)(2,1)S(1)}, bf16[256,1024]{1,0:T(8,128)(2,1)S(1)}, u32[]{:S(2)}, u32[]{:S(2)}) collective-permute-start(bf16[256,1024]{1,0:T(8,128)(2,1)S(1)} %get-tuple-element.19.rest_5_), channel_id=1, source_target_pairs={{0,4},{4,8},{8,12},{12,16},{16,20},{20,24},{24,28},{28,0},{64,68},... | collective-permute-start | bytes 1572872 | tf_op jit(solution)/shard_map/ppermute | solution.py:23
  17.9 18.2 %collective-permute-start.16 = (bf16[256,1024]{1,0:T(8,128)(2,1)S(1)}, bf16[256,1024]{1,0:T(8,128)(2,1)}, u32[]{:S(2)}, u32[]{:S(2)}) collective-permute-start(bf16[256,1024]{1,0:T(8,128)(2,1)S(1)} %collective-permute-done.12.rest_13_), channel_id=1, source_target_pairs={{0,28},{4,0},{8,4},{12,8},{16,12},{20,16},{24,20},{28,24},{64,92},... | collective-permute-start | bytes 1572872 | tf_op jit(solution)/shard_map/ppermute | solution.py:23
  25.2 22.1 %collective-permute-start.9 = (bf16[256,1024]{1,0:T(8,128)(2,1)S(1)}, bf16[256,1024]{1,0:T(8,128)(2,1)S(1)}, u32[]{:S(2)}, u32[]{:S(2)}) collective-permute-start(bf16[256,1024]{1,0:T(8,128)(2,1)S(1)} %get-tuple-element.19.rest_5_), channel_id=1, source_target_pairs={{0,28},{4,0},{8,4},{12,8},{16,12},{20,16},{24,20},{28,24},{64,92},... | collective-permute-start | bytes 1572872 | tf_op jit(solution)/shard_map/ppermute | solution.py:23
  28.5 42.9 %collective-permute-start.4 = (bf16[4,128,1024]{2,1,0:T(8,128)(2,1)}, bf16[4,128,1024]{2,1,0:T(8,128)(2,1)}, u32[]{:S(2)}, u32[]{:S(2)}) collective-permute-start(bf16[4,128,1024]{2,1,0:T(8,128)(2,1)} %pad_maximum_fusion.first), channel_id=1, source_target_pairs={{0,1},{1,0},{64,65},{65,64},{2,3},{3,2},{66,67},{67,66},{4,5},{5,4... | collective-permute-start | bytes 3145736 | tf_op jit(solution)/shard_map/ppermute | solution.py:33
  30.2 22.2 %collective-permute-start.13 = (bf16[256,1024]{1,0:T(8,128)(2,1)S(1)}, bf16[256,1024]{1,0:T(8,128)(2,1)S(1)}, u32[]{:S(2)}, u32[]{:S(2)}) collective-permute-start(bf16[256,1024]{1,0:T(8,128)(2,1)S(1)} %collective-permute-done.12.rest_13_), channel_id=1, source_target_pairs={{0,4},{4,8},{8,12},{12,16},{16,20},{20,24},{24,28},{28,0},{64,68},... | collective-permute-start | bytes 1572872 | tf_op jit(solution)/shard_map/ppermute | solution.py:23
  31.3 26.2 %collective-permute-start.6 = (bf16[256,1024]{1,0:T(8,128)(2,1)S(1)}, bf16[256,1024]{1,0:T(8,128)(2,1)S(1)}, u32[]{:S(2)}, u32[]{:S(2)}) collective-permute-start(bf16[256,1024]{1,0:T(8,128)(2,1)S(1)} %collective-permute-done.5.rest_6_), channel_id=1, source_target_pairs={{0,4},{4,8},{8,12},{12,16},{16,20},{20,24},{24,28},{28,0},{64,68},... | collective-permute-start | bytes 1572872 | tf_op jit(solution)/shard_map/ppermute | solution.py:23
  36.1 22.6 %collective-permute-start.17 = (bf16[256,1024]{1,0:T(8,128)(2,1)}, bf16[256,1024]{1,0:T(8,128)(2,1)}, u32[]{:S(2)}, u32[]{:S(2)}) collective-permute-start(bf16[256,1024]{1,0:T(8,128)(2,1)} %collective-permute-done.16.rest_20_), channel_id=1, source_target_pairs={{0,28},{4,0},{8,4},{12,8},{16,12},{20,16},{24,20},{28,24},{64,92},... | collective-permute-start | bytes 1572872 | tf_op jit(solution)/shard_map/ppermute | solution.py:23
  47.3 22.5 %collective-permute-start.10 = (bf16[256,1024]{1,0:T(8,128)(2,1)S(1)}, bf16[256,1024]{1,0:T(8,128)(2,1)}, u32[]{:S(2)}, u32[]{:S(2)}) collective-permute-start(bf16[256,1024]{1,0:T(8,128)(2,1)S(1)} %collective-permute-done.9.rest_12_), channel_id=1, source_target_pairs={{0,28},{4,0},{8,4},{12,8},{16,12},{20,16},{24,20},{28,24},{64,92},... | collective-permute-start | bytes 1572872 | tf_op jit(solution)/shard_map/ppermute | solution.py:23
  52.4 22.9 %collective-permute-start.14 = (bf16[256,1024]{1,0:T(8,128)(2,1)S(1)}, bf16[256,1024]{1,0:T(8,128)(2,1)}, u32[]{:S(2)}, u32[]{:S(2)}) collective-permute-start(bf16[256,1024]{1,0:T(8,128)(2,1)S(1)} %collective-permute-done.13.rest_14_), channel_id=1, source_target_pairs={{0,4},{4,8},{8,12},{12,16},{16,20},{20,24},{24,28},{28,0},{64,68},... | collective-permute-start | bytes 1572872 | tf_op jit(solution)/shard_map/ppermute | solution.py:23
  57.5 22.3 %collective-permute-start.7 = (bf16[256,1024]{1,0:T(8,128)(2,1)S(1)}, bf16[256,1024]{1,0:T(8,128)(2,1)}, u32[]{:S(2)}, u32[]{:S(2)}) collective-permute-start(bf16[256,1024]{1,0:T(8,128)(2,1)S(1)} %collective-permute-done.6.rest_7_), channel_id=1, source_target_pairs={{0,4},{4,8},{8,12},{12,16},{16,20},{20,24},{24,28},{28,0},{64,68},... | collective-permute-start | bytes 1572872 | tf_op jit(solution)/shard_map/ppermute | solution.py:23
  58.6 22.5 %collective-permute-start.18 = (bf16[256,1024]{1,0:T(8,128)(2,1)}, bf16[256,1024]{1,0:T(8,128)(2,1)}, u32[]{:S(2)}, u32[]{:S(2)}) collective-permute-start(bf16[256,1024]{1,0:T(8,128)(2,1)} %collective-permute-done.17.rest_19_), channel_id=1, source_target_pairs={{0,28},{4,0},{8,4},{12,8},{16,12},{20,16},{24,20},{28,24},{64,92},... | collective-permute-start | bytes 1572872 | tf_op jit(solution)/shard_map/ppermute | solution.py:23
  69.8 33.3 %collective-permute-start.55 = (bf16[4,128,1024]{2,1,0:T(8,128)(2,1)}, bf16[4,128,1024]{2,1,0:T(8,128)(2,1)}, u32[]{:S(2)}, u32[]{:S(2)}) collective-permute-start(bf16[4,128,1024]{2,1,0:T(8,128)(2,1)} %pad_maximum_fusion.2.first), channel_id=1, source_target_pairs={{0,1},{1,0},{64,65},{65,64},{2,3},{3,2},{66,67},{67,66},{4,5},{5,4... | collective-permute-start | bytes 3145736 | tf_op jit(solution)/shard_map/ppermute | solution.py:33
  71.4 20.9 %collective-permute-start.11 = (bf16[256,1024]{1,0:T(8,128)(2,1)}, bf16[256,1024]{1,0:T(8,128)(2,1)}, u32[]{:S(2)}, u32[]{:S(2)}) collective-permute-start(bf16[256,1024]{1,0:T(8,128)(2,1)} %collective-permute-done.10.rest_11_), channel_id=1, source_target_pairs={{0,28},{4,0},{8,4},{12,8},{16,12},{20,16},{24,20},{28,24},{64,92},... | collective-permute-start | bytes 1572872 | tf_op jit(solution)/shard_map/ppermute | solution.py:23
  75.3 17.0 %collective-permute-start.15 = (bf16[256,1024]{1,0:T(8,128)(2,1)}, bf16[256,1024]{1,0:T(8,128)(2,1)}, u32[]{:S(2)}, u32[]{:S(2)}) collective-permute-start(bf16[256,1024]{1,0:T(8,128)(2,1)} %collective-permute-done.14.rest_15_), channel_id=1, source_target_pairs={{0,4},{4,8},{8,12},{12,16},{16,20},{20,24},{24,28},{28,0},{64,68},... | collective-permute-start | bytes 1572872 | tf_op jit(solution)/shard_map/ppermute | solution.py:23
  79.7 20.2 %collective-permute-start.8 = (bf16[256,1024]{1,0:T(8,128)(2,1)}, bf16[256,1024]{1,0:T(8,128)(2,1)}, u32[]{:S(2)}, u32[]{:S(2)}) collective-permute-start(bf16[256,1024]{1,0:T(8,128)(2,1)} %collective-permute-done.7.rest_8_), channel_id=1, source_target_pairs={{0,4},{4,8},{8,12},{12,16},{16,20},{20,24},{24,28},{28,0},{64,68},... | collective-permute-start | bytes 1572872 | tf_op jit(solution)/shard_map/ppermute | solution.py:23
  81.1 20.5 %collective-permute-start.19 = (bf16[256,1024]{1,0:T(8,128)(2,1)}, bf16[256,1024]{1,0:T(8,128)(2,1)}, u32[]{:S(2)}, u32[]{:S(2)}) collective-permute-start(bf16[256,1024]{1,0:T(8,128)(2,1)} %collective-permute-done.18.rest_18_), channel_id=1, source_target_pairs={{0,28},{4,0},{8,4},{12,8},{16,12},{20,16},{24,20},{28,24},{64,92},... | collective-permute-start | bytes 1572872 | tf_op jit(solution)/shard_map/ppermute | solution.py:23
  112.7 16.8 %collective-permute-start.37 = (bf16[256,1024]{1,0:T(8,128)(2,1)S(1)}, bf16[256,1024]{1,0:T(8,128)(2,1)S(1)}, u32[]{:S(2)}, u32[]{:S(2)}) collective-permute-start(bf16[256,1024]{1,0:T(8,128)(2,1)S(1)} %get-tuple-element.19.rest_5_), channel_id=1, source_target_pairs={{128,160},{130,162},{160,128},{162,130},{192,224},{194,226},{224,1... | collective-permute-start | bytes 1572872 | tf_op jit(solution)/shard_map/ppermute | solution.py:28
  123.4 16.7 %collective-permute-start.35 = (bf16[256,1024]{1,0:T(8,128)(2,1)S(1)}, bf16[256,1024]{1,0:T(8,128)(2,1)S(1)}, u32[]{:S(2)}, u32[]{:S(2)}) collective-permute-start(bf16[256,1024]{1,0:T(8,128)(2,1)S(1)} %copy-done.6), channel_id=1, source_target_pairs={{128,156},{132,128},{136,132},{140,136},{144,140},{148,144},{152,1... | collective-permute-start | bytes 1572872 | tf_op jit(solution)/shard_map/ppermute | solution.py:23
  140.1 20.3 %collective-permute-start.28 = (bf16[2,128,1024]{2,1,0:T(8,128)(2,1)S(1)}, bf16[2,128,1024]{2,1,0:T(8,128)(2,1)S(1)}, u32[]{:S(2)}, u32[]{:S(2)}) collective-permute-start(bf16[2,128,1024]{2,1,0:T(8,128)(2,1)S(1)} %get-tuple-element.82), channel_id=1, source_target_pairs={{128,130},{130,128},{160,162},{162,160},{129,131},{131,129},{161,1... | collective-permute-start | bytes 1572872 | tf_op jit(solution)/shard_map/ppermute | solution.py:28
  147.9 18.7 %collective-permute-start.36 = (bf16[256,1024]{1,0:T(8,128)(2,1)S(1)}, bf16[256,1024]{1,0:T(8,128)(2,1)S(1)}, u32[]{:S(2)}, u32[]{:S(2)}) collective-permute-start(bf16[256,1024]{1,0:T(8,128)(2,1)S(1)} %collective-permute-done.35.rest_28_), channel_id=1, source_target_pairs={{128,156},{132,128},{136,132},{140,136},{144,140},{148,144},{152,1... | collective-permute-start | bytes 1572872 | tf_op jit(solution)/shard_map/ppermute | solution.py:23
  152.5 17.4 %collective-permute-start.32 = (bf16[256,1024]{1,0:T(8,128)(2,1)S(1)}, bf16[256,1024]{1,0:T(8,128)(2,1)S(1)}, u32[]{:S(2)}, u32[]{:S(2)}) collective-permute-start(bf16[256,1024]{1,0:T(8,128)(2,1)S(1)} %collective-permute-done.31.rest_23_), channel_id=1, source_target_pairs={{128,132},{132,136},{136,140},{140,144},{144,148},{148,152},{152,1... | collective-permute-start | bytes 1572872 | tf_op jit(solution)/shard_map/ppermute | solution.py:23
  154.5 18.4 %collective-permute-start.42 = (bf16[256,1024]{1,0:T(8,128)(2,1)S(1)}, bf16[256,1024]{1,0:T(8,128)(2,1)S(1)}, u32[]{:S(2)}, u32[]{:S(2)}) collective-permute-start(bf16[256,1024]{1,0:T(8,128)(2,1)S(1)} %collective-permute-done.41.rest_36_), channel_id=1, source_target_pairs={{128,156},{132,128},{136,132},{140,136},{144,140},{148,144},{152,1... | collective-permute-start | bytes 1572872 | tf_op jit(solution)/shard_map/ppermute | solution.py:23
  159.7 18.7 %collective-permute-start.64 = (bf16[2,128,1024]{2,1,0:T(8,128)(2,1)S(1)}, bf16[2,128,1024]{2,1,0:T(8,128)(2,1)S(1)}, u32[]{:S(2)}, u32[]{:S(2)}) collective-permute-start(bf16[2,128,1024]{2,1,0:T(8,128)(2,1)S(1)} %get-tuple-element.84), channel_id=1, source_target_pairs={{128,130},{130,128},{160,162},{162,160},{129,131},{131,129},{161,1... | collective-permute-start | bytes 1572872 | tf_op jit(solution)/shard_map/ppermute | solution.py:28
  160.5 20.8 %collective-permute-start.38 = (bf16[256,1024]{1,0:T(8,128)(2,1)S(1)}, bf16[256,1024]{1,0:T(8,128)(2,1)S(1)}, u32[]{:S(2)}, u32[]{:S(2)}) collective-permute-start(bf16[256,1024]{1,0:T(8,128)(2,1)S(1)} %collective-permute-done.5.rest_6_), channel_id=1, source_target_pairs={{128,160},{130,162},{160,128},{162,130},{192,224},{194,226},{224,1... | collective-permute-start | bytes 1572872 | tf_op jit(solution)/shard_map/ppermute | solution.py:28
  166.7 19.2 %collective-permute-start.39 = (bf16[256,1024]{1,0:T(8,128)(2,1)S(1)}, bf16[256,1024]{1,0:T(8,128)(2,1)S(1)}, u32[]{:S(2)}, u32[]{:S(2)}) collective-permute-start(bf16[256,1024]{1,0:T(8,128)(2,1)S(1)} %collective-permute-done.6.rest_7_), channel_id=1, source_target_pairs={{128,160},{130,162},{160,128},{162,130},{192,224},{194,226},{224,1... | collective-permute-start | bytes 1572872 | tf_op jit(solution)/shard_map/ppermute | solution.py:28
  169.9 21.0 %collective-permute-start.33 = (bf16[256,1024]{1,0:T(8,128)(2,1)S(1)}, bf16[256,1024]{1,0:T(8,128)(2,1)}, u32[]{:S(2)}, u32[]{:S(2)}) collective-permute-start(bf16[256,1024]{1,0:T(8,128)(2,1)S(1)} %collective-permute-done.32.rest_24_), channel_id=1, source_target_pairs={{128,132},{132,136},{136,140},{140,144},{144,148},{148,152},{152,1... | collective-permute-start | bytes 1572872 | tf_op jit(solution)/shard_map/ppermute | solution.py:23
  172.9 20.0 %collective-permute-start.43 = (bf16[256,1024]{1,0:T(8,128)(2,1)S(1)}, bf16[256,1024]{1,0:T(8,128)(2,1)}, u32[]{:S(2)}, u32[]{:S(2)}) collective-permute-start(bf16[256,1024]{1,0:T(8,128)(2,1)S(1)} %collective-permute-done.42.rest_35_), channel_id=1, source_target_pairs={{128,156},{132,128},{136,132},{140,136},{144,140},{148,144},{152,1... | collective-permute-start | bytes 1572872 | tf_op jit(solution)/shard_map/ppermute | solution.py:23
  178.5 26.9 %collective-permute-start.29 = (bf16[2,2,128,1024]{3,2,1,0:T(8,128)(2,1)}, bf16[2,2,128,1024]{3,2,1,0:T(8,128)(2,1)}, u32[]{:S(2)}, u32[]{:S(2)}) collective-permute-start(bf16[2,2,128,1024]{3,2,1,0:T(8,128)(2,1)} %pad_maximum_fusion.1.rest_3_), channel_id=1, source_target_pairs={{128,129},{129,128},{130,131},{131,130},{132,133},{133,132},{134,1... | collective-permute-start | bytes 3145736 | tf_op jit(solution)/shard_map/ppermute | solution.py:33
  181.2 26.1 %collective-permute-start.65 = (bf16[2,2,128,1024]{3,2,1,0:T(8,128)(2,1)}, bf16[2,2,128,1024]{3,2,1,0:T(8,128)(2,1)}, u32[]{:S(2)}, u32[]{:S(2)}) collective-permute-start(bf16[2,2,128,1024]{3,2,1,0:T(8,128)(2,1)} %pad_maximum_fusion.3.rest_3_), channel_id=1, source_target_pairs={{128,129},{129,128},{130,131},{131,130},{132,133},{133,132},{134,1... | collective-permute-start | bytes 3145736 | tf_op jit(solution)/shard_map/ppermute | solution.py:33
  210.8 120.1 %collective-permute-start.47 = (bf16[128,1024]{1,0:T(8,128)(2,1)S(1)}, bf16[128,1024]{1,0:T(8,128)(2,1)S(1)}, u32[]{:S(2)}, u32[]{:S(2)}) collective-permute-start(bf16[128,1024]{1,0:T(8,128)(2,1)S(1)} %fusion.15), channel_id=1, source_target_pairs={{128,192},{129,193},{130,194},{131,195},{132,196},{133,197},{134,1... | collective-permute-start | bytes 786440 | tf_op jit(solution)/shard_map/ppermute | solution.py:37
  212.3 124.3 %collective-permute-start.68 = (bf16[128,1024]{1,0:T(8,128)(2,1)S(1)}, bf16[128,1024]{1,0:T(8,128)(2,1)S(1)}, u32[]{:S(2)}, u32[]{:S(2)}) collective-permute-start(bf16[128,1024]{1,0:T(8,128)(2,1)S(1)} %fusion.7), channel_id=1, source_target_pairs={{128,192},{129,193},{130,194},{131,195},{132,196},{133,197},{134,1... | collective-permute-start | bytes 786440 | tf_op jit(solution)/shard_map/ppermute | solution.py:37
  (96 other events, 1797.0 us)
